TPU v7x, 256 devices: a whole 4x4x8 slice. The times are simulated.
256 devices in a mesh: seq: 128 (over z, x, y), head: 2 (over core).
Axes of the slice: x: 4, y: 4, z: 8, core: 2. Of those that a mesh axis runs over, the one named last changes fastest.
Arguments:
- query_rows: bfloat16 [16384, 2048], P('seq', 'head'), may hold values from -6 to 6
- key_rows: bfloat16 [16384, 2048], P('seq', 'head'), may hold values from -6 to 6
- value_rows: bfloat16 [16384, 2048], P('seq', 'head'), may hold values from -6 to 6
- doc_lengths: int32 [128], replicated, may hold values from 1 to 1920, 16384 in all
- norm_gain: float32 [128], replicated, may hold values from 0.25 to 1.75
- out_weight: bfloat16 [2048, 2048], P('head'), may hold values from -0.125 to 0.125
Outputs:
- layer_out: bfloat16 [16384, 2048], P('seq', 'head')
Inputs may be any that keep to these rules, and one draw needn't show every extreme that they name: `doc_lengths`: positive lengths summing to 16384; the longest has exactly 1920 tokens.
All inputs are finite; a program needn't handle non-finite values.
Results may differ from a plain program's by a relative error of at most 0.0049.
Values sent between devices are 32-bit elements; how exact they have to be, the bound alone decides.
A program may use at most 320 MiB of HBM per device.

v0:
```python
import jax
import jax.numpy as jnp
from jax import lax
from jax.sharding import PartitionSpec as P

HEAD_DIM = 128
ITERS = 4


epsilon = 1e-06
damping = 1.0
highest = lax.Precision.HIGHEST


def carried_in(part, axis, combine, identity):
    place = lax.axis_index(axis)
    gathered = jax.tree.map(lambda a: lax.all_gather(a, axis), part)
    state = jax.tree.map(lambda a, e: jnp.zeros_like(a) + jnp.asarray(e, a.dtype), part, identity)

    def one(step, state):
        return combine(
            state, jax.tree.map(lambda a: lax.dynamic_index_in_dim(a, step, 0, False), gathered)
        )

    return lax.fori_loop(0, place, one, state)


def unit_rows(matrix_rows):
    matrix_rows = matrix_rows.astype(jnp.float32)
    return matrix_rows * lax.rsqrt(
        jnp.sum(matrix_rows * matrix_rows, axis=-1, keepdims=True) + epsilon
    )


def document_ids(doc_lengths, positions):
    starts = jnp.cumsum(doc_lengths, dtype=jnp.int32) - doc_lengths
    below = (starts[None, :] <= positions[:, None]).astype(jnp.int32)
    return jnp.sum(below, axis=1, dtype=jnp.int32) - 1


def apply_state(vector, prefix_state, carried, mask, key_block, target):
    from_prefix = (
        jnp.einsum("htj,hij->hti", vector, prefix_state, precision=highest) * carried[None, :, None]
    )
    scores = jnp.einsum("htj,hsj->hts", vector, key_block, precision=highest) * mask[None]
    return from_prefix + jnp.einsum("hts,hsi->hti", scores, target, precision=highest)


def solve_block(queries, key_block, value_block, gram, cross, carried, mask):
    solution = jnp.zeros_like(queries)
    residual = queries
    direction = queries
    norm_now = jnp.sum(residual * residual, axis=-1, keepdims=True)
    for iteration in range(ITERS):
        product_image = (
            apply_state(direction, gram, carried, mask, key_block, key_block) + damping * direction
        )
        step_size = norm_now / (
            jnp.sum(direction * product_image, axis=-1, keepdims=True) + epsilon
        )
        solution = solution + step_size * direction
        residual = residual - step_size * product_image
        norm_next = jnp.sum(residual * residual, axis=-1, keepdims=True)
        direction = residual + norm_next / (norm_now + epsilon) * direction
        norm_now = norm_next
    return apply_state(solution, cross, carried, mask, key_block, value_block)


def combine_states(earlier, latter):
    carry_on = (1 - latter[2]).astype(jnp.float32)
    return (
        latter[0] + carry_on * earlier[0],
        latter[1] + carry_on * earlier[1],
        jnp.maximum(earlier[2], latter[2]),
    )


def on_device(query_rows, key_rows, value_rows, doc_lengths, norm_gain, out_weight):
    tokens_here = query_rows.shape[0]
    heads_here = query_rows.shape[1] // HEAD_DIM

    def heads_first(matrix_rows):
        return matrix_rows.reshape(tokens_here, heads_here, HEAD_DIM).transpose(1, 0, 2)

    queries = unit_rows(heads_first(query_rows))
    keys_here = unit_rows(heads_first(key_rows))
    values = heads_first(value_rows).astype(jnp.float32)
    shard_index = lax.axis_index("seq")
    offsets = jnp.arange(tokens_here, dtype=jnp.int32)
    positions = shard_index * tokens_here + offsets
    doc_ids = document_ids(doc_lengths, positions)
    previous = document_ids(doc_lengths, positions[:1] - 1)[0]
    carried = (doc_ids == previous).astype(jnp.float32)
    restart = (doc_ids[-1] != previous).astype(jnp.int32)
    tail_mask = (doc_ids == doc_ids[-1]).astype(jnp.float32)
    tail_gram = jnp.einsum(
        "hsi,hsj->hij", keys_here * tail_mask[None, :, None], keys_here, precision=highest
    )
    tail_cross = jnp.einsum(
        "hsi,hsj->hij", values * tail_mask[None, :, None], keys_here, precision=highest
    )
    empty_state = jnp.zeros_like(tail_gram)
    gram, cross, unused = carried_in(
        (tail_gram, tail_cross, restart),
        "seq",
        combine_states,
        (empty_state, empty_state, jnp.int32(0)),
    )
    causal = offsets[None, :] <= offsets[:, None]
    mask = ((doc_ids[:, None] == doc_ids[None, :]) & causal).astype(jnp.float32)
    mixed_heads = solve_block(queries, keys_here, values, gram, cross, carried, mask)
    inverse_rms = lax.rsqrt(jnp.mean(mixed_heads * mixed_heads, axis=-1, keepdims=True) + epsilon)
    normed = (mixed_heads * inverse_rms * norm_gain).astype(jnp.bfloat16)
    normed = normed.transpose(1, 0, 2).reshape(tokens_here, heads_here * HEAD_DIM)
    partial_out = jnp.dot(normed, out_weight, preferred_element_type=jnp.float32)
    return lax.psum_scatter(partial_out, "head", scatter_dimension=1, tiled=True).astype(
        jnp.bfloat16
    )


def solution(mesh):
    in_specs = (P("seq", "head"), P("seq", "head"), P("seq", "head"), P(), P(), P("head", None))
    out_specs = P("seq", "head")
    return jax.shard_map(
        on_device, mesh=mesh, in_specs=in_specs, out_specs=out_specs, check_vma=False
    )
```

profile of v0, /device:TPU:225, one launch (start us, length us, event | category | flops | bytes accessed | tf_op | source)
XLA Modules:
  0.0 1098.6 jit_solution(17859523635387270049)
XLA Ops:
  13.4 2.0 fusion.11
  15.5 2.0 fusion.7
  21.4 18.5 %all-reduce = s32[128]{0:T(128)S(1)} all-reduce(s32[128]{0:T(128)S(1)} %dynamic-update-slice), channel_id=1, replica_groups=mesh['seq'=128,'head'=2] {'seq'}, use_global_device_ids=true, to_apply=%add | all-reduce | flops 128 | bytes 1024
  41.0 312.2 %all-gather.7.cloned.1.call-done = f32[1024,128,128]{2,1,0:T(8,128)} async-done(((f32[8,128,128]{2,1,0:T(8,128)}), f32[1024,128,128]{2,1,0:T(8,128)}) %all-gather.7.cloned.1.call-update) | async-done | bytes 67108880 | tf_op jit(solution)/shard_map/all_gather | solution.py:17
  353.2 340.3 %all-gather.5.cloned.1.call-done = f32[1024,128,128]{2,1,0:T(8,128)} async-done(((f32[8,128,128]{2,1,0:T(8,128)}), f32[1024,128,128]{2,1,0:T(8,128)}) %all-gather.5.cloned.1.call-update) | async-done | bytes 67108880 | tf_op jit(solution)/shard_map/all_gather | solution.py:17
  693.6 323.0 %while.14 = (s32[]{:T(128)}, f32[8,128,128]{2,1,0:T(8,128)S(1)}, f32[8,128,128]{2,1,0:T(8,128)S(1)}, s32[]{:T(128)}, f32[128,8,128,128]{3,2,1,0:T(8,128)}, /*ind...) while((s32[]{:T(128)}, f32[8,128,128]{2,1,0:T(8,128)S(1)}, ...), condition=%wide.region_7.8_spmd, body=%wide.region_6.7_spmd.sunk | while | flops 524295 | bytes 3145911 | solution.py:25
  695.0 1.5 bitcast_add_fusion.3
  697.9 1.5 bitcast_add_fusion.3
  700.7 1.5 bitcast_add_fusion.3
  703.6 1.5 bitcast_add_fusion.3
  706.5 1.5 bitcast_add_fusion.3
  712.3 1.5 bitcast_add_fusion.3
  715.2 1.5 bitcast_add_fusion.3
  718.0 1.5 bitcast_add_fusion.3
  720.9 1.5 bitcast_add_fusion.3
  726.7 1.5 bitcast_add_fusion.3
  732.4 1.5 bitcast_add_fusion.3
  735.3 1.5 bitcast_add_fusion.3
  738.2 1.5 bitcast_add_fusion.3
  741.1 1.5 bitcast_add_fusion.3
  746.9 1.5 bitcast_add_fusion.3
  1031.6 3.9 fusion.24
  1035.5 54.8 %reduce-scatter.2.cloned.1.call-done = f32[128,1024]{1,0:T(8,128)} async-done(((f32[128,2048]{1,0:T(8,128)}), f32[128,1024]{1,0:T(8,128)}) %reduce-scatter.2.cloned.1.call-update) | async-done | bytes 524304 | tf_op jit(solution)/shard_map/reduce_scatter | solution.py:116
  1090.3 1.8 convert_element_type.77
  (268 shorter events, 244.6 us)
Async XLA Ops:
  6.5 346.7 %all-gather.7.cloned.1.call-start = ((), (), s32[]{:S(2)}) async-start(), calls=%async_computation.3 | async-start | bytes 67633152 | tf_op jit(solution)/shard_map/all_gather | solution.py:17
  15.4 678.1 %all-gather.5.cloned.1.call-start = ((), (), s32[]{:S(2)}) async-start(), calls=%async_computation.2 | async-start | bytes 67633152 | tf_op jit(solution)/shard_map/all_gather | solution.py:17
  17.5 1072.8 %reduce-scatter.2.cloned.1.call-start = ((), (), s32[]{:S(2)}) async-start(), calls=%async_computation.1 | async-start | bytes 1572864 | tf_op jit(solution)/shard_map/reduce_scatter | solution.py:116
Sparse Core Ops, SparseCore 0:
  15.6 337.6 all-gather.6
  356.7 336.7 all-gather.4
  1035.7 54.6 reduce-scatter.1
where the time goes:
time: 1110 us; the launch traced here: 1100 us
  waiting for transfers between devices  707 us (64%)
  other arithmetic  173 us (16%)
  local copies, waits for them, and re-layouts  81.8 us (7%)
  loops' own time  81.5 us (7%)
  matrix products  22 us (2%)
  blocking collectives  18.5 us (2%)
  between operations  14.8 us (1%)
    all_gather x2, waiting for transfers between devices, carried_in(): gathered = jax.tree.map(lambda a: lax.all_gather(a, axis), part)  652 us
    add x112, other arithmetic, combine_states(): latter[1] + carry_on * earlier[1]  166 us
    another operation x1, loops' own time, carried_in(): return lax.fori_loop(0, place, one, state)  81.5 us
    dynamic_slice x112, local copies, waits for them, and re-layouts, one(): lax.dynamic_index_in_dim(a, step, 0, False)  75.1 us
    reduce_scatter x1, waiting for transfers between devices, on_device(): lax.psum_scatter(partial_out, 'head', scatter_dimension=1, tiled=True)  54.8 us
  transfers between devices with their start and end apart: 3, of which 3 were waited for; matrix products, arithmetic and copies ran while one was open for 1% of the time, Pallas kernels for 0%

commit v1 on v0

v1 whole, which is shorter than its diff:
```python
import functools

import jax
import jax.numpy as jnp
from jax import lax
from jax.experimental import pallas as pl
from jax.experimental.pallas import tpu as pltpu
from jax.sharding import PartitionSpec as P

MESH = pl.DeviceIdType.MESH
F32 = jnp.float32
BF16 = jnp.bfloat16
HD = 128
TOK = 128
HEADS = 8
PAIRS = 4
ITERS = 4
CH = 64
NB = 4
epsilon = 1e-06
damping = 1.0

WR, WZ, WC, WP, WE, WEC = 0, 4, 8, 12, 16, 32


def split2(a):
    hi = a.astype(BF16)
    return hi, (a - hi.astype(F32)).astype(BF16)


def dot(a, b, dims):
    return lax.dot_general(a, b, (dims, ((), ())), preferred_element_type=F32)


NN, NT, TN = ((1,), (0,)), ((1,), (1,)), ((0,), (0,))


def kernel(
    q_hbm, k_hbm, v_hbm, len_ref, gain_ref, w_hbm, out_ref,
    q_ref, k_ref, v_ref, w_ref,
    tbuf, ybuf, rbuf, zs, zr, eo, ebuf, xs, nbuf, acc, other,
    mask_ref, ksr, wts, tail_ref, car_ref,
    lsem, ys, yr, xsd, xr, zsd, zrv, es, er, ps, pr,
):
    s = lax.axis_index("seq")
    c = lax.axis_index("head")
    y = lax.rem(s, 4)
    row = s - y
    x = lax.rem(s // 4, 4)
    col = s - 4 * x
    z = s // 16

    def at_y(d):
        return row + lax.rem(y + d, 4)

    def at_x(d):
        return col + 4 * lax.rem(x + d, 4)

    def at_z(d):
        return lax.rem(s + 16 * d + 128, 128)

    loads = [
        pltpu.make_async_copy(k_hbm, k_ref, lsem.at[0]),
        pltpu.make_async_copy(v_hbm, v_ref, lsem.at[1]),
        pltpu.make_async_copy(q_hbm, q_ref, lsem.at[2]),
        pltpu.make_async_copy(w_hbm, w_ref, lsem.at[3]),
    ]
    for cp in loads:
        cp.start()

    barrier = pltpu.get_barrier_semaphore()
    for d in (1, 2, 3):
        pl.semaphore_signal(barrier, inc=1, device_id=(at_y(d), c), device_id_type=MESH)
        pl.semaphore_signal(barrier, inc=1, device_id=(at_x(d), c), device_id_type=MESH)
    pl.semaphore_signal(barrier, inc=1, device_id=(at_z(-1), c), device_id_type=MESH)
    pl.semaphore_signal(barrier, inc=1, device_id=(s, 1 - c), device_id_type=MESH)

    lrow = len_ref[...].astype(F32)
    ri = lax.broadcasted_iota(jnp.int32, (TOK, TOK), 0)
    ci = lax.broadcasted_iota(jnp.int32, (TOK, TOK), 1)
    lcol = jnp.sum(jnp.where(ri == ci, lrow, 0.0), axis=1, keepdims=True)
    srow = jnp.sum(jnp.where(ri < ci, lcol, 0.0), axis=0, keepdims=True)
    scol = jnp.sum(jnp.where(ci < ri, lrow, 0.0), axis=1, keepdims=True)
    base = (s * TOK).astype(F32)
    rf, cf = ri.astype(F32), ci.astype(F32)
    doc_col = jnp.sum(jnp.where(srow <= base + rf, 1.0, 0.0), axis=1, keepdims=True)
    doc_row = jnp.sum(jnp.where(scol <= base + cf, 1.0, 0.0), axis=0, keepdims=True)
    ends = jnp.sum(jnp.where(scol <= cf * TOK + (TOK - 1.0), 1.0, 0.0), axis=0, keepdims=True)
    shard = lax.broadcasted_iota(jnp.int32, (1, TOK), 1)

    def end_of(i):
        return jnp.sum(jnp.where(shard == i, ends, 0.0), axis=1, keepdims=True)

    def put(k, flag):
        wts[k : k + 1, :] = jnp.broadcast_to(jnp.where(flag, 1.0, 0.0), (1, HD))

    here, before = end_of(s), end_of(s - 1)
    car_ref[...] = jnp.broadcast_to(jnp.where(doc_col == before, 1.0, 0.0), (TOK, HD))
    tail_ref[...] = jnp.broadcast_to(jnp.where(doc_col == here, 1.0, 0.0), (TOK, HD))
    mask_ref[...] = jnp.where((doc_col == doc_row) & (ci <= ri), 1.0, 0.0)
    dy = [end_of(row + i) for i in range(4)]
    dx = [end_of(16 * z + 4 * i + 3) for i in range(4)]
    dprev, dplane = end_of(row - 1), end_of(16 * z - 1)
    for i in range(4):
        put(WR + i, dy[i] == dy[3])
        put(WZ + i, dx[i] == dx[3])
        put(WC + i, (dx[i] == dprev) & (jnp.full((1, 1), i, jnp.int32) < x))
    put(WP, (dplane == dprev) & (dplane > 0.0))
    for t in range(1, 4):
        for i in range(t):
            put(WE + 4 * t + i, dy[i] == dy[t - 1])
        put(WEC + t, dprev == dy[t - 1])

    def wt(k):
        return wts[k : k + 1, :]

    def head_cols(h):
        return pl.ds(pl.multiple_of(h * HD, HD), HD)

    def ycopy(st, d):
        return pltpu.make_async_remote_copy(
            tbuf.at[st, lax.rem(y + d, 4)], ybuf.at[st, y], ys.at[st, d - 1], yr.at[st, d - 1],
            device_id=(at_y(d), c), device_id_type=MESH,
        )

    def xcopy(st, d):
        return pltpu.make_async_remote_copy(
            rbuf.at[st, x], rbuf.at[st, x], xsd.at[st, d - 1], xr.at[st, d - 1],
            device_id=(at_x(d), c), device_id_type=MESH,
        )

    def zcopy(st):
        return pltpu.make_async_remote_copy(
            zs.at[st], zr.at[st], zsd.at[st], zrv.at[st],
            device_id=(at_z(1), c), device_id_type=MESH,
        )

    def ecopy(st, d):
        return pltpu.make_async_remote_copy(
            eo.at[st, lax.rem(y + d, 4)], ebuf.at[st, y], es.at[st, d - 1], er.at[st, d - 1],
            device_id=(at_y(d), c), device_id_type=MESH,
        )

    def send_tail(st):
        ybuf[st, y] = tbuf[st, y]
        for d in (1, 2, 3):
            ycopy(st, d).start()

    loads[0].wait()

    def gram_stage(g, carry):
        for i in range(2):
            h = 2 * g + i
            k = k_ref[:, head_cols(h)]
            kf = k.astype(F32)
            ks = lax.rsqrt(jnp.sum(kf * kf, axis=1, keepdims=True) + epsilon)
            ksr[pl.ds(h, 1), :] = jnp.sum(jnp.where(ri == ci, ks, 0.0), axis=0, keepdims=True)
            hi, lo = split2(kf * (ks * ks) * tail_ref[...])
            gram = dot(jnp.concatenate([hi, lo], 0), jnp.concatenate([k, k], 0), TN)
            tbuf[g, 2 * i] = gram[:CH]
            tbuf[g, 2 * i + 1] = gram[CH:]
        return carry

    def cross_stage(g, carry):
        for i in range(2):
            h = 2 * g + i
            k = k_ref[:, head_cols(h)]
            v = v_ref[:, head_cols(h)]
            kf = k.astype(F32)
            ks = lax.rsqrt(jnp.sum(kf * kf, axis=1, keepdims=True) + epsilon)
            hi, lo = split2(kf * ks * tail_ref[...])
            cross = dot(jnp.concatenate([hi, lo], 0), jnp.concatenate([v, v], 0), TN)
            tbuf[PAIRS + g, 2 * i] = cross[:CH]
            tbuf[PAIRS + g, 2 * i + 1] = cross[CH:]
        send_tail(PAIRS + g)
        return carry

    gram_stage(0, 0)
    pl.semaphore_wait(barrier, 8)
    send_tail(0)

    def gram_send(g, carry):
        gram_stage(g, carry)
        send_tail(g)
        return carry

    lax.fori_loop(1, PAIRS, gram_send, 0)
    loads[1].wait()
    lax.fori_loop(0, PAIRS, cross_stage, 0)

    def row_sum(st, carry):
        for d in (1, 2, 3):
            ycopy(st, d).wait_recv()
        total = ybuf[st, 3]
        for i in range(3):
            total = total + wt(WR + i) * ybuf[st, i]
        rbuf[st, x] = total
        for d in (1, 2, 3):
            xcopy(st, d).start()
        return carry

    def plane_sum(st, carry):
        for d in (1, 2, 3):
            xcopy(st, d).wait_recv()
        total = rbuf[st, 3]
        for i in range(3):
            total = total + wt(WZ + i) * rbuf[st, i]
        zs[st] = total
        zcopy(st).start()
        return carry

    def give_back(st, carry):
        zcopy(st).wait_recv()
        come = wt(WP) * zr[st]
        for i in range(3):
            come = come + wt(WC + i) * rbuf[st, i]
        eo[st, 0] = come
        parts = [ybuf[st, i] for i in range(3)]
        for t in range(1, 4):
            total = wt(WEC + t) * come
            for i in range(t):
                total = total + wt(WE + 4 * t + i) * parts[i]
            eo[st, t] = total
        ebuf[st, y] = eo[st, y]
        for d in (1, 2, 3):
            ecopy(st, d).start()
        return carry

    def solve(g, carry):
        for d in (1, 2, 3):
            ecopy(g, d).wait_recv()
        car = car_ref[...]
        car16 = car.astype(BF16)
        state = []
        for i in range(2):
            h = 2 * g + i
            q = q_ref[:, head_cols(h)].astype(F32)
            qn = q * lax.rsqrt(jnp.sum(q * q, axis=1, keepdims=True) + epsilon)
            k = k_ref[:, head_cols(h)]
            gram = jnp.concatenate([ebuf[g, 2 * i], ebuf[g, 2 * i + 1]], 0)
            ghi, glo = split2(gram)
            ksrow = ksr[pl.ds(h, 1), :]
            state.append(
                dict(
                    kk=jnp.concatenate([k, k], 1),
                    rhs=jnp.concatenate([ghi, ghi, glo, k, k], 0),
                    m=mask_ref[...] * (ksrow * ksrow),
                    x=None, r=qn, p=qn, n=jnp.sum(qn * qn, axis=1, keepdims=True),
                )
            )
        for it in range(ITERS):
            for e in state:
                p = e["p"]
                hi, lo = split2(p)
                sc = dot(jnp.concatenate([hi, lo], 1), e["kk"], NT) * e["m"]
                shi, slo = split2(sc)
                chi = hi * car16
                lhs = jnp.concatenate([chi, lo * car16, chi, shi, slo], 1)
                a = dot(lhs, e["rhs"], NN) + damping * p
                alpha = e["n"] / (jnp.sum(p * a, axis=1, keepdims=True) + epsilon)
                e["x"] = alpha * p if e["x"] is None else e["x"] + alpha * p
                if it < ITERS - 1:
                    e["r"] = e["r"] - alpha * a
                    new = jnp.sum(e["r"] * e["r"], axis=1, keepdims=True)
                    e["p"] = e["r"] + new / (e["n"] + epsilon) * p
                    e["n"] = new
        for i in range(2):
            xs[2 * g + i] = state[i]["x"]
        return carry

    def finish(g, carry):
        st = PAIRS + g
        for d in (1, 2, 3):
            ecopy(st, d).wait_recv()
        car16 = car_ref[...].astype(BF16)
        for i in range(2):
            h = 2 * g + i
            k = k_ref[:, head_cols(h)]
            v = v_ref[:, head_cols(h)]
            cross = jnp.concatenate([ebuf[st, 2 * i], ebuf[st, 2 * i + 1]], 0)
            xhi, xlo = split2(cross)
            hi, lo = split2(xs[h])
            m = mask_ref[...] * ksr[pl.ds(h, 1), :]
            sc = dot(jnp.concatenate([hi, lo], 1), jnp.concatenate([k, k], 1), NT) * m
            shi, slo = split2(sc)
            chi = hi * car16
            lhs = jnp.concatenate([chi, lo * car16, chi, shi, slo], 1)
            mixed = dot(lhs, jnp.concatenate([xhi, xhi, xlo, v, v], 0), NN)
            inv = lax.rsqrt(jnp.sum(mixed * mixed, axis=1, keepdims=True) / HD + epsilon)
            nbuf[:, head_cols(h)] = (mixed * inv * gain_ref[...]).astype(BF16)
        return carry

    lax.fori_loop(0, PAIRS, row_sum, 0)
    lax.fori_loop(0, PAIRS, plane_sum, 0)
    lax.fori_loop(0, PAIRS, give_back, 0)
    lax.fori_loop(PAIRS, 2 * PAIRS, row_sum, 0)
    lax.fori_loop(PAIRS, 2 * PAIRS, plane_sum, 0)
    lax.fori_loop(PAIRS, 2 * PAIRS, give_back, 0)
    loads[2].wait()
    lax.fori_loop(0, PAIRS, solve, 0)
    lax.fori_loop(0, PAIRS, finish, 0)

    loads[3].wait()
    half = HEADS * HD
    width = half // NB

    def pcopy(b):
        return pltpu.make_async_remote_copy(
            acc.at[b], other.at[b], ps.at[b], pr.at[b],
            device_id=(s, 1 - c), device_id_type=MESH,
        )

    normed = nbuf[...]
    for b in range(NB):
        cols = pl.ds(pl.multiple_of((1 - c) * half + b * width, width), width)
        acc[b] = dot(normed, w_ref[:, cols], NN)
        pcopy(b).start()
    for b in range(NB):
        cols = pl.ds(pl.multiple_of(c * half + b * width, width), width)
        mine = dot(normed, w_ref[:, cols], NN)
        pcopy(b).wait_recv()
        out_ref[:, b * width : (b + 1) * width] = (mine + other[b]).astype(BF16)

    def drain(st, carry):
        for d in (1, 2, 3):
            ycopy(st, d).wait_send()
            xcopy(st, d).wait_send()
            ecopy(st, d).wait_send()
        zcopy(st).wait_send()
        return carry

    lax.fori_loop(0, 2 * PAIRS, drain, 0)
    for b in range(NB):
        pcopy(b).wait_send()


def on_device(query_rows, key_rows, value_rows, doc_lengths, norm_gain, out_weight):
    half = HEADS * HD
    st = 2 * PAIRS
    dma = pltpu.SemaphoreType.DMA
    vm = pl.BlockSpec(memory_space=pltpu.VMEM)
    anywhere = pl.BlockSpec(memory_space=pl.ANY)
    return pl.pallas_call(
        kernel,
        out_shape=jax.ShapeDtypeStruct((TOK, half), BF16),
        in_specs=[anywhere, anywhere, anywhere, vm, vm, anywhere],
        out_specs=vm,
        scratch_shapes=[
            pltpu.VMEM((TOK, half), BF16),
            pltpu.VMEM((TOK, half), BF16),
            pltpu.VMEM((TOK, half), BF16),
            pltpu.VMEM((half, 2 * half), BF16),
            pltpu.VMEM((st, 4, CH, HD), F32),
            pltpu.VMEM((st, 4, CH, HD), F32),
            pltpu.VMEM((st, 4, CH, HD), F32),
            pltpu.VMEM((st, CH, HD), F32),
            pltpu.VMEM((st, CH, HD), F32),
            pltpu.VMEM((st, 4, CH, HD), F32),
            pltpu.VMEM((st, 4, CH, HD), F32),
            pltpu.VMEM((HEADS, TOK, HD), F32),
            pltpu.VMEM((TOK, half), BF16),
            pltpu.VMEM((NB, TOK, half // NB), F32),
            pltpu.VMEM((NB, TOK, half // NB), F32),
            pltpu.VMEM((TOK, TOK), F32),
            pltpu.VMEM((HEADS, HD), F32),
            pltpu.VMEM((40, HD), F32),
            pltpu.VMEM((TOK, HD), F32),
            pltpu.VMEM((TOK, HD), F32),
            dma((4,)),
            dma((st, 3)), dma((st, 3)),
            dma((st, 3)), dma((st, 3)),
            dma((st,)), dma((st,)),
            dma((st, 3)), dma((st, 3)),
            dma((NB,)), dma((NB,)),
        ],
        compiler_params=pltpu.CompilerParams(collective_id=0, has_side_effects=True),
        name="mesa",
    )(
        query_rows, key_rows, value_rows,
        doc_lengths.reshape(1, -1), norm_gain.reshape(1, -1), out_weight,
    )


def solution(mesh):
    in_specs = (P("seq", "head"), P("seq", "head"), P("seq", "head"), P(), P(), P("head", None))
    return jax.shard_map(
        on_device, mesh=mesh, in_specs=in_specs, out_specs=P("seq", "head"), check_vma=False
    )
```

time: 1110 us -> 53 us (0.05)
  the two profiles are of different devices: /device:TPU:225 before, /device:TPU:1 now
where the time goes in v1:
time: 53 us; the launch traced here: 52.9 us
  Pallas kernels  51.2 us (97%)
  local copies, waits for them, and re-layouts  1.67 us (3%)
    pallas_call x1, Pallas kernels, on_device(): pl.pallas_call(kernel, out_shape=jax.ShapeDtypeStruct((TOK, half), BF16),...  51.2 us
    unnamed x1, local copies, waits for them, and re-layouts  1.67 us

profile of v1, /device:TPU:1, one launch (start us, length us, event | category | flops | bytes accessed | tf_op | source)
XLA Modules:
  0.0 52.9 jit_solution(6858228451288216095)
XLA Ops:
  0.0 51.2 %mesa.1 = bf16[128,1024]{1,0:T(8,128)(2,1)} custom-call(bf16[128,1024]{1,0:T(8,128)(2,1)} %q_hbm.1, bf16[128,1024]{1,0:T(8,128)(2,1)} %k_hbm.1, bf16[128,1024]{1,0:T(8,128)(2,1)} %v_hbm.1, s32[1,128]{1,0:T(1,128)} %bitcast.2, f32[1,128]{1,0:T(1,128)} %bitcast.3, bf16[1024,2048]{1,0:T(8,128)(2,1)} %w_hbm.1), custom_call_target="tpu_custom_call" | custom-call | tf_op jit(solution)/shard_map/mesa/pallas_call | solution.py:343
  51.2 1.7 %copy.8 = bf16[128,1024]{1,0:T(8,128)(2,1)} copy(bf16[128,1024]{1,0:T(8,128)(2,1)} %mesa.1) | data formatting | bytes 524288

commit v2 on v1

--- a/solution.py
+++ b/solution.py
@@ -16,6 +16,8 @@
 PAIRS = 4
 ITERS = 4
 CH = 64
+CG = 40
+LAST = 7
 NB = 4
 epsilon = 1e-06
 damping = 1.0
@@ -40,7 +42,7 @@
     q_ref, k_ref, v_ref, w_ref,
     tbuf, ybuf, rbuf, zs, zr, eo, ebuf, xs, nbuf, acc, other,
     mask_ref, ksr, wts, tail_ref, car_ref,
-    lsem, ys, yr, xsd, xr, zsd, zrv, es, er, ps, pr,
+    lsem, ys, yr, xsd, xr, zsd, zrv, es, er, ps, pr, ready,
 ):
     s = lax.axis_index("seq")
     c = lax.axis_index("head")
@@ -56,24 +58,28 @@
     def at_x(d):
         return col + 4 * lax.rem(x + d, 4)
 
-    def at_z(d):
-        return lax.rem(s + 16 * d + 128, 128)
-
     loads = [
         pltpu.make_async_copy(k_hbm, k_ref, lsem.at[0]),
         pltpu.make_async_copy(v_hbm, v_ref, lsem.at[1]),
         pltpu.make_async_copy(q_hbm, q_ref, lsem.at[2]),
         pltpu.make_async_copy(w_hbm, w_ref, lsem.at[3]),
     ]
-    for cp in loads:
-        cp.start()
-
     barrier = pltpu.get_barrier_semaphore()
     for d in (1, 2, 3):
         pl.semaphore_signal(barrier, inc=1, device_id=(at_y(d), c), device_id_type=MESH)
         pl.semaphore_signal(barrier, inc=1, device_id=(at_x(d), c), device_id_type=MESH)
-    pl.semaphore_signal(barrier, inc=1, device_id=(at_z(-1), c), device_id_type=MESH)
     pl.semaphore_signal(barrier, inc=1, device_id=(s, 1 - c), device_id_type=MESH)
+
+    @pl.when(z < LAST)
+    def _():
+        pl.semaphore_signal(barrier, inc=1, device_id=(s + 16, c), device_id_type=MESH)
+
+    for cp in loads:
+        cp.start()
+
+    @pl.when(z == 0)
+    def _():
+        zr[...] = jnp.zeros_like(zr)
 
     lrow = len_ref[...].astype(F32)
     ri = lax.broadcasted_iota(jnp.int32, (TOK, TOK), 0)
@@ -117,51 +123,74 @@
     def head_cols(h):
         return pl.ds(pl.multiple_of(h * HD, HD), HD)
 
+    def rows(st):
+        return pl.ds(0, CG if st < PAIRS else CH)
+
     def ycopy(st, d):
+        r = rows(st)
         return pltpu.make_async_remote_copy(
-            tbuf.at[st, lax.rem(y + d, 4)], ybuf.at[st, y], ys.at[st, d - 1], yr.at[st, d - 1],
+            tbuf.at[st, lax.rem(y + d, 4), r], ybuf.at[st, y, r],
+            ys.at[st, d - 1], yr.at[st, d - 1],
             device_id=(at_y(d), c), device_id_type=MESH,
         )
 
     def xcopy(st, d):
+        r = rows(st)
         return pltpu.make_async_remote_copy(
-            rbuf.at[st, x], rbuf.at[st, x], xsd.at[st, d - 1], xr.at[st, d - 1],
+            rbuf.at[st, x, r], rbuf.at[st, x, r], xsd.at[st, d - 1], xr.at[st, d - 1],
             device_id=(at_x(d), c), device_id_type=MESH,
         )
 
     def zcopy(st):
+        r = rows(st)
         return pltpu.make_async_remote_copy(
-            zs.at[st], zr.at[st], zsd.at[st], zrv.at[st],
-            device_id=(at_z(1), c), device_id_type=MESH,
+            zs.at[st, r], zr.at[st, r], zsd.at[st], zrv.at[st],
+            device_id=(lax.rem(s + 16, 128), c), device_id_type=MESH,
         )
 
     def ecopy(st, d):
+        r = rows(st)
         return pltpu.make_async_remote_copy(
-            eo.at[st, lax.rem(y + d, 4)], ebuf.at[st, y], es.at[st, d - 1], er.at[st, d - 1],
+            eo.at[st, lax.rem(y + d, 4), r], ebuf.at[st, y, r],
+            es.at[st, d - 1], er.at[st, d - 1],
             device_id=(at_y(d), c), device_id_type=MESH,
         )
 
     def send_tail(st):
-        ybuf[st, y] = tbuf[st, y]
+        r = rows(st)
         for d in (1, 2, 3):
             ycopy(st, d).start()
-
-    loads[0].wait()
-
-    def gram_stage(g, carry):
-        for i in range(2):
-            h = 2 * g + i
+        ybuf[st, y, r] = tbuf[st, y, r]
+
+    lane = lax.broadcasted_iota(jnp.int32, (32, HD), 1)
+
+    def gram_stage(g):
+        grams = []
+        for h in (2 * g, 2 * g + 1):
             k = k_ref[:, head_cols(h)]
             kf = k.astype(F32)
             ks = lax.rsqrt(jnp.sum(kf * kf, axis=1, keepdims=True) + epsilon)
-            ksr[pl.ds(h, 1), :] = jnp.sum(jnp.where(ri == ci, ks, 0.0), axis=0, keepdims=True)
+            ksr[h : h + 1, :] = jnp.sum(jnp.where(ri == ci, ks, 0.0), axis=0, keepdims=True)
             hi, lo = split2(kf * (ks * ks) * tail_ref[...])
-            gram = dot(jnp.concatenate([hi, lo], 0), jnp.concatenate([k, k], 0), TN)
-            tbuf[g, 2 * i] = gram[:CH]
-            tbuf[g, 2 * i + 1] = gram[CH:]
-        return carry
-
-    def cross_stage(g, carry):
+            grams.append(dot(jnp.concatenate([hi, lo], 0), jnp.concatenate([k, k], 0), TN))
+        blocks = []
+        for gram in grams:
+            blocks.append(gram[:32])
+            blocks.append(jnp.where(lane < 32, pltpu.roll(gram[96:], 32, 1), gram[32:64]))
+        blocks.append(jnp.where(lane < 64, pltpu.roll(grams[1][64:96], 64, 1), grams[0][64:96]))
+        packed = jnp.concatenate(blocks, 0)
+        for o in range(4):
+            tbuf[g, o, :CG] = packed[CG * o : CG * (o + 1)]
+
+    def gram_of(g, i):
+        packed = jnp.concatenate([ebuf[g, o, :CG] for o in range(4)], 0)
+        first, second, third = packed[64 * i : 64 * i + 32], packed[64 * i + 32 : 64 * i + 64], packed[128:]
+        if i == 1:
+            third = pltpu.roll(third, 64, 1)
+        upper = jnp.concatenate([first, second, third, pltpu.roll(second, 96, 1)], 0)
+        return jnp.where(ci // 32 >= ri // 32, upper, upper.T)
+
+    def cross_stage(g):
         for i in range(2):
             h = 2 * g + i
             k = k_ref[:, head_cols(h)]
@@ -172,61 +201,55 @@
             cross = dot(jnp.concatenate([hi, lo], 0), jnp.concatenate([v, v], 0), TN)
             tbuf[PAIRS + g, 2 * i] = cross[:CH]
             tbuf[PAIRS + g, 2 * i + 1] = cross[CH:]
-        send_tail(PAIRS + g)
-        return carry
-
-    gram_stage(0, 0)
-    pl.semaphore_wait(barrier, 8)
-    send_tail(0)
-
-    def gram_send(g, carry):
-        gram_stage(g, carry)
-        send_tail(g)
-        return carry
-
-    lax.fori_loop(1, PAIRS, gram_send, 0)
-    loads[1].wait()
-    lax.fori_loop(0, PAIRS, cross_stage, 0)
-
-    def row_sum(st, carry):
+
+    def row_sum(st):
+        r = rows(st)
         for d in (1, 2, 3):
             ycopy(st, d).wait_recv()
-        total = ybuf[st, 3]
+        total = ybuf[st, 3, r]
         for i in range(3):
-            total = total + wt(WR + i) * ybuf[st, i]
-        rbuf[st, x] = total
+            total = total + wt(WR + i) * ybuf[st, i, r]
+        rbuf[st, x, r] = total
         for d in (1, 2, 3):
             xcopy(st, d).start()
-        return carry
-
-    def plane_sum(st, carry):
+
+    def plane_sum(st):
+        r = rows(st)
         for d in (1, 2, 3):
             xcopy(st, d).wait_recv()
-        total = rbuf[st, 3]
+        total = rbuf[st, 3, r]
         for i in range(3):
-            total = total + wt(WZ + i) * rbuf[st, i]
-        zs[st] = total
-        zcopy(st).start()
-        return carry
-
-    def give_back(st, carry):
-        zcopy(st).wait_recv()
-        come = wt(WP) * zr[st]
+            total = total + wt(WZ + i) * rbuf[st, i, r]
+        zs[st, r] = total
+
+        @pl.when(z < LAST)
+        def _():
+            if st == 0:
+                pl.semaphore_wait(ready, 1)
+            zcopy(st).start()
+
+    def give_back(st):
+        r = rows(st)
+
+        @pl.when(z > 0)
+        def _():
+            zcopy(st).wait_recv()
+
+        come = wt(WP) * zr[st, r]
         for i in range(3):
-            come = come + wt(WC + i) * rbuf[st, i]
-        eo[st, 0] = come
-        parts = [ybuf[st, i] for i in range(3)]
+            come = come + wt(WC + i) * rbuf[st, i, r]
+        eo[st, 0, r] = come
+        parts = [ybuf[st, i, r] for i in range(3)]
         for t in range(1, 4):
             total = wt(WEC + t) * come
             for i in range(t):
                 total = total + wt(WE + 4 * t + i) * parts[i]
-            eo[st, t] = total
-        ebuf[st, y] = eo[st, y]
+            eo[st, t, r] = total
         for d in (1, 2, 3):
             ecopy(st, d).start()
-        return carry
-
-    def solve(g, carry):
+        ebuf[st, y, r] = eo[st, y, r]
+
+    def solve(g):
         for d in (1, 2, 3):
             ecopy(g, d).wait_recv()
         car = car_ref[...]
@@ -237,9 +260,8 @@
             q = q_ref[:, head_cols(h)].astype(F32)
             qn = q * lax.rsqrt(jnp.sum(q * q, axis=1, keepdims=True) + epsilon)
             k = k_ref[:, head_cols(h)]
-            gram = jnp.concatenate([ebuf[g, 2 * i], ebuf[g, 2 * i + 1]], 0)
-            ghi, glo = split2(gram)
-            ksrow = ksr[pl.ds(h, 1), :]
+            ghi, glo = split2(gram_of(g, i))
+            ksrow = ksr[h : h + 1, :]
             state.append(
                 dict(
                     kk=jnp.concatenate([k, k], 1),
@@ -266,9 +288,8 @@
                     e["n"] = new
         for i in range(2):
             xs[2 * g + i] = state[i]["x"]
-        return carry
-
-    def finish(g, carry):
+
+    def finish(g):
         st = PAIRS + g
         for d in (1, 2, 3):
             ecopy(st, d).wait_recv()
@@ -280,7 +301,7 @@
             cross = jnp.concatenate([ebuf[st, 2 * i], ebuf[st, 2 * i + 1]], 0)
             xhi, xlo = split2(cross)
             hi, lo = split2(xs[h])
-            m = mask_ref[...] * ksr[pl.ds(h, 1), :]
+            m = mask_ref[...] * ksr[h : h + 1, :]
             sc = dot(jnp.concatenate([hi, lo], 1), jnp.concatenate([k, k], 1), NT) * m
             shi, slo = split2(sc)
             chi = hi * car16
@@ -288,17 +309,42 @@
             mixed = dot(lhs, jnp.concatenate([xhi, xhi, xlo, v, v], 0), NN)
             inv = lax.rsqrt(jnp.sum(mixed * mixed, axis=1, keepdims=True) / HD + epsilon)
             nbuf[:, head_cols(h)] = (mixed * inv * gain_ref[...]).astype(BF16)
-        return carry
-
-    lax.fori_loop(0, PAIRS, row_sum, 0)
-    lax.fori_loop(0, PAIRS, plane_sum, 0)
-    lax.fori_loop(0, PAIRS, give_back, 0)
-    lax.fori_loop(PAIRS, 2 * PAIRS, row_sum, 0)
-    lax.fori_loop(PAIRS, 2 * PAIRS, plane_sum, 0)
-    lax.fori_loop(PAIRS, 2 * PAIRS, give_back, 0)
+
+    loads[0].wait()
+    gram_stage(0)
+    pl.semaphore_wait(barrier, 7 + jnp.minimum(z, 1))
+
+    @pl.when(z > 0)
+    def _():
+        pl.semaphore_signal(ready, inc=1, device_id=(s - 16, c), device_id_type=MESH)
+
+    send_tail(0)
+    for g in range(1, PAIRS):
+        gram_stage(g)
+        send_tail(g)
+    loads[1].wait()
+    for g in range(PAIRS):
+        cross_stage(g)
+        send_tail(PAIRS + g)
+    for t in range(2 * PAIRS):
+        row_sum(t)
+        if t >= 2:
+            plane_sum(t - 2)
+        if t >= 4:
+            give_back(t - 4)
     loads[2].wait()
-    lax.fori_loop(0, PAIRS, solve, 0)
-    lax.fori_loop(0, PAIRS, finish, 0)
+    plane_sum(6)
+    give_back(4)
+    solve(0)
+    plane_sum(7)
+    give_back(5)
+    solve(1)
+    give_back(6)
+    give_back(7)
+    solve(2)
+    solve(3)
+    for g in range(PAIRS):
+        finish(g)
 
     loads[3].wait()
     half = HEADS * HD
@@ -321,15 +367,17 @@
         pcopy(b).wait_recv()
         out_ref[:, b * width : (b + 1) * width] = (mine + other[b]).astype(BF16)
 
-    def drain(st, carry):
+    for st in range(2 * PAIRS):
         for d in (1, 2, 3):
             ycopy(st, d).wait_send()
             xcopy(st, d).wait_send()
             ecopy(st, d).wait_send()
-        zcopy(st).wait_send()
-        return carry
-
-    lax.fori_loop(0, 2 * PAIRS, drain, 0)
+
+    @pl.when(z < LAST)
+    def _():
+        for st in range(2 * PAIRS):
+            zcopy(st).wait_send()
+
     for b in range(NB):
         pcopy(b).wait_send()
 
@@ -372,6 +420,7 @@
             dma((st,)), dma((st,)),
             dma((st, 3)), dma((st, 3)),
             dma((NB,)), dma((NB,)),
+            pltpu.SemaphoreType.REGULAR,
         ],
         compiler_params=pltpu.CompilerParams(collective_id=0, has_side_effects=True),
         name="mesa",

time: 53 us -> 39.5 us (0.75)
  the two profiles are of different devices: /device:TPU:1 before, /device:TPU:225 now
where the time goes in v2:
time: 39.5 us; the launch traced here: 39.3 us
  Pallas kernels  37.6 us (95%)
  local copies, waits for them, and re-layouts  1.67 us (4%)
    pallas_call x1, Pallas kernels, on_device(): pl.pallas_call(kernel, out_shape=jax.ShapeDtypeStruct((TOK, half), BF16),...  37.6 us
    unnamed x1, local copies, waits for them, and re-layouts  1.67 us

profile of v2, /device:TPU:225, one launch (start us, length us, event | category | flops | bytes accessed | tf_op | source)
XLA Modules:
  0.0 39.3 jit_solution(6256421030646421683)
XLA Ops:
  0.0 37.6 %mesa.1 = bf16[128,1024]{1,0:T(8,128)(2,1)} custom-call(bf16[128,1024]{1,0:T(8,128)(2,1)} %q_hbm.1, bf16[128,1024]{1,0:T(8,128)(2,1)} %k_hbm.1, bf16[128,1024]{1,0:T(8,128)(2,1)} %v_hbm.1, s32[1,128]{1,0:T(1,128)} %bitcast.2, f32[1,128]{1,0:T(1,128)} %bitcast.3, bf16[1024,2048]{1,0:T(8,128)(2,1)} %w_hbm.1), custom_call_target="tpu_custom_call" | custom-call | tf_op jit(solution)/shard_map/mesa/pallas_call | solution.py:391
  37.7 1.7 %copy.8 = bf16[128,1024]{1,0:T(8,128)(2,1)} copy(bf16[128,1024]{1,0:T(8,128)(2,1)} %mesa.1) | data formatting | bytes 524288

commit v3 on v2

--- a/solution.py
+++ b/solution.py
@@ -1,5 +1,3 @@
-import functools
-
 import jax
 import jax.numpy as jnp
 from jax import lax
@@ -38,9 +36,9 @@
 
 
 def kernel(
-    q_hbm, k_hbm, v_hbm, len_ref, gain_ref, w_hbm, out_ref,
-    q_ref, k_ref, v_ref, w_ref,
-    tbuf, ybuf, rbuf, zs, zr, eo, ebuf, xs, nbuf, acc, other,
+    q_hbm, k_hbm, v_hbm, len_hbm, gain_hbm, w_hbm, out_ref,
+    q_ref, k_ref, v_ref, w_ref, len_ref, gain_ref,
+    tbuf, ybuf, rbuf, zs, zr, eo, ebuf, qs, scq, rhs, xl, nbuf, acc, other,
     mask_ref, ksr, wts, tail_ref, car_ref,
     lsem, ys, yr, xsd, xr, zsd, zrv, es, er, ps, pr, ready,
 ):
@@ -58,12 +56,6 @@
     def at_x(d):
         return col + 4 * lax.rem(x + d, 4)
 
-    loads = [
-        pltpu.make_async_copy(k_hbm, k_ref, lsem.at[0]),
-        pltpu.make_async_copy(v_hbm, v_ref, lsem.at[1]),
-        pltpu.make_async_copy(q_hbm, q_ref, lsem.at[2]),
-        pltpu.make_async_copy(w_hbm, w_ref, lsem.at[3]),
-    ]
     barrier = pltpu.get_barrier_semaphore()
     for d in (1, 2, 3):
         pl.semaphore_signal(barrier, inc=1, device_id=(at_y(d), c), device_id_type=MESH)
@@ -74,6 +66,16 @@
     def _():
         pl.semaphore_signal(barrier, inc=1, device_id=(s + 16, c), device_id_type=MESH)
 
+    loads = [
+        pltpu.make_async_copy(a, b, lsem.at[i])
+        for i, (a, b) in enumerate(
+            [
+                (len_hbm, len_ref), (k_hbm, k_ref), (v_hbm, v_ref),
+                (q_hbm, q_ref), (gain_hbm, gain_ref), (w_hbm, w_ref),
+            ]
+        )
+    ]
+    LEN, KEY, VAL, QUERY, GAIN, WEIGHT = loads
     for cp in loads:
         cp.start()
 
@@ -81,6 +83,7 @@
     def _():
         zr[...] = jnp.zeros_like(zr)
 
+    LEN.wait()
     lrow = len_ref[...].astype(F32)
     ri = lax.broadcasted_iota(jnp.int32, (TOK, TOK), 0)
     ci = lax.broadcasted_iota(jnp.int32, (TOK, TOK), 1)
@@ -249,68 +252,102 @@
             ecopy(st, d).start()
         ebuf[st, y, r] = eo[st, y, r]
 
+    def prepare(g):
+        for h in (2 * g, 2 * g + 1):
+            q = q_ref[:, head_cols(h)].astype(F32)
+            qn = q * lax.rsqrt(jnp.sum(q * q, axis=1, keepdims=True) + epsilon)
+            k = k_ref[:, head_cols(h)]
+            hi, lo = split2(qn)
+            qs[h] = qn
+            scq[h] = dot(jnp.concatenate([hi, lo], 1), jnp.concatenate([k, k], 1), NT)
+            khi, klo = split2(dot(k, k, NT))
+            both = jnp.concatenate([k, khi], 1)
+            rhs[h, 3 * HD : 4 * HD] = both
+            rhs[h, 4 * HD : 5 * HD] = both
+            rhs[h, 5 * HD :] = jnp.concatenate([jnp.zeros_like(klo), klo], 1)
+
     def solve(g):
         for d in (1, 2, 3):
             ecopy(g, d).wait_recv()
-        car = car_ref[...]
-        car16 = car.astype(BF16)
+        car16 = car_ref[...].astype(BF16)
         state = []
         for i in range(2):
             h = 2 * g + i
-            q = q_ref[:, head_cols(h)].astype(F32)
-            qn = q * lax.rsqrt(jnp.sum(q * q, axis=1, keepdims=True) + epsilon)
             k = k_ref[:, head_cols(h)]
             ghi, glo = split2(gram_of(g, i))
+            shi, slo = split2(dot(jnp.concatenate([ghi, glo], 1), jnp.concatenate([k, k], 1), NT))
+            both = jnp.concatenate([ghi, shi], 1)
+            rhs[h, :HD] = both
+            rhs[h, HD : 2 * HD] = both
+            rhs[h, 2 * HD : 3 * HD] = jnp.concatenate([glo, slo], 1)
             ksrow = ksr[h : h + 1, :]
+            qn, sc = qs[h], scq[h]
             state.append(
                 dict(
-                    kk=jnp.concatenate([k, k], 1),
-                    rhs=jnp.concatenate([ghi, ghi, glo, k, k], 0),
-                    m=mask_ref[...] * (ksrow * ksrow),
-                    x=None, r=qn, p=qn, n=jnp.sum(qn * qn, axis=1, keepdims=True),
+                    h=h, m=mask_ref[...] * (ksrow * ksrow), p=qn, sp=sc, r=qn, sr=sc,
+                    n=jnp.sum(qn * qn, axis=1, keepdims=True),
                 )
             )
         for it in range(ITERS):
+            last = it == ITERS - 1
             for e in state:
-                p = e["p"]
+                p, sp = e["p"], e["sp"]
                 hi, lo = split2(p)
-                sc = dot(jnp.concatenate([hi, lo], 1), e["kk"], NT) * e["m"]
-                shi, slo = split2(sc)
+                shi, slo = split2(sp * e["m"])
                 chi = hi * car16
-                lhs = jnp.concatenate([chi, lo * car16, chi, shi, slo], 1)
-                a = dot(lhs, e["rhs"], NN) + damping * p
+                lhs = jnp.concatenate([chi, lo * car16, chi, shi, slo, shi], 1)
+                if last:
+                    a = dot(lhs[:, : 5 * HD], rhs[e["h"], : 5 * HD, :HD], NN) + damping * p
+                else:
+                    both = dot(lhs, rhs[e["h"]], NN)
+                    a, sa = both[:, :HD] + damping * p, both[:, HD:] + damping * sp
                 alpha = e["n"] / (jnp.sum(p * a, axis=1, keepdims=True) + epsilon)
-                e["x"] = alpha * p if e["x"] is None else e["x"] + alpha * p
-                if it < ITERS - 1:
+                e["x"] = alpha * p if it == 0 else e["x"] + alpha * p
+                e["sx"] = alpha * sp if it == 0 else e["sx"] + alpha * sp
+                if not last:
                     e["r"] = e["r"] - alpha * a
+                    e["sr"] = e["sr"] - alpha * sa
                     new = jnp.sum(e["r"] * e["r"], axis=1, keepdims=True)
-                    e["p"] = e["r"] + new / (e["n"] + epsilon) * p
+                    beta = new / (e["n"] + epsilon)
+                    e["p"] = e["r"] + beta * p
+                    e["sp"] = e["sr"] + beta * sp
                     e["n"] = new
-        for i in range(2):
-            xs[2 * g + i] = state[i]["x"]
+        for e in state:
+            h = e["h"]
+            hi, lo = split2(e["x"])
+            shi, slo = split2(e["sx"] * (mask_ref[...] * ksr[h : h + 1, :]))
+            chi = hi * car16
+            xl[h] = jnp.concatenate([chi, lo * car16, chi, shi, slo], 1)
 
     def finish(g):
         st = PAIRS + g
         for d in (1, 2, 3):
             ecopy(st, d).wait_recv()
-        car16 = car_ref[...].astype(BF16)
         for i in range(2):
             h = 2 * g + i
-            k = k_ref[:, head_cols(h)]
             v = v_ref[:, head_cols(h)]
             cross = jnp.concatenate([ebuf[st, 2 * i], ebuf[st, 2 * i + 1]], 0)
             xhi, xlo = split2(cross)
-            hi, lo = split2(xs[h])
-            m = mask_ref[...] * ksr[h : h + 1, :]
-            sc = dot(jnp.concatenate([hi, lo], 1), jnp.concatenate([k, k], 1), NT) * m
-            shi, slo = split2(sc)
-            chi = hi * car16
-            lhs = jnp.concatenate([chi, lo * car16, chi, shi, slo], 1)
-            mixed = dot(lhs, jnp.concatenate([xhi, xhi, xlo, v, v], 0), NN)
+            mixed = dot(xl[h], jnp.concatenate([xhi, xhi, xlo, v, v], 0), NN)
             inv = lax.rsqrt(jnp.sum(mixed * mixed, axis=1, keepdims=True) / HD + epsilon)
             nbuf[:, head_cols(h)] = (mixed * inv * gain_ref[...]).astype(BF16)
 
-    loads[0].wait()
+    half = HEADS * HD
+    width = half // NB
+
+    def columns(b):
+        side = 1 - c if b < NB else c
+        return pl.ds(pl.multiple_of(side * half + (b % NB) * width, width), width)
+
+    def project(g, b):
+        mine = slice(2 * HD * g, 2 * HD * (g + 1))
+        return dot(nbuf[:, mine], w_ref[mine, columns(b)], NN)
+
+    def project_pair(g):
+        for b in range(2 * NB):
+            acc[b] = project(g, b) if g == 0 else acc[b] + project(g, b)
+
+    KEY.wait()
     gram_stage(0)
     pl.semaphore_wait(barrier, 7 + jnp.minimum(z, 1))
 
@@ -322,33 +359,49 @@
     for g in range(1, PAIRS):
         gram_stage(g)
         send_tail(g)
-    loads[1].wait()
+    VAL.wait()
     for g in range(PAIRS):
         cross_stage(g)
         send_tail(PAIRS + g)
-    for t in range(2 * PAIRS):
-        row_sum(t)
-        if t >= 2:
-            plane_sum(t - 2)
-        if t >= 4:
-            give_back(t - 4)
-    loads[2].wait()
-    plane_sum(6)
+    row_sum(0)
+    row_sum(1)
+    QUERY.wait()
+    prepare(0)
+    row_sum(2)
+    row_sum(3)
+    plane_sum(0)
+    prepare(1)
+    plane_sum(1)
+    row_sum(4)
+    plane_sum(2)
+    give_back(0)
+    plane_sum(3)
+    row_sum(5)
+    give_back(1)
+    prepare(2)
+    row_sum(6)
+    give_back(2)
+    plane_sum(4)
+    give_back(3)
+    prepare(3)
+    row_sum(7)
+    plane_sum(5)
     give_back(4)
     solve(0)
+    plane_sum(6)
+    give_back(5)
     plane_sum(7)
-    give_back(5)
     solve(1)
     give_back(6)
     give_back(7)
     solve(2)
     solve(3)
-    for g in range(PAIRS):
+    GAIN.wait()
+    WEIGHT.wait()
+    for g in range(PAIRS - 1):
         finish(g)
-
-    loads[3].wait()
-    half = HEADS * HD
-    width = half // NB
+        project_pair(g)
+    finish(PAIRS - 1)
 
     def pcopy(b):
         return pltpu.make_async_remote_copy(
@@ -356,14 +409,11 @@
             device_id=(s, 1 - c), device_id_type=MESH,
         )
 
-    normed = nbuf[...]
     for b in range(NB):
-        cols = pl.ds(pl.multiple_of((1 - c) * half + b * width, width), width)
-        acc[b] = dot(normed, w_ref[:, cols], NN)
+        acc[b] = acc[b] + project(PAIRS - 1, b)
         pcopy(b).start()
     for b in range(NB):
-        cols = pl.ds(pl.multiple_of(c * half + b * width, width), width)
-        mine = dot(normed, w_ref[:, cols], NN)
+        mine = acc[NB + b] + project(PAIRS - 1, NB + b)
         pcopy(b).wait_recv()
         out_ref[:, b * width : (b + 1) * width] = (mine + other[b]).astype(BF16)
 
@@ -390,14 +440,16 @@
     anywhere = pl.BlockSpec(memory_space=pl.ANY)
     return pl.pallas_call(
         kernel,
-        out_shape=jax.ShapeDtypeStruct((TOK, half), BF16),
-        in_specs=[anywhere, anywhere, anywhere, vm, vm, anywhere],
+        out_shape=pltpu.VMEM((TOK, half), BF16),
+        in_specs=[anywhere] * 6,
         out_specs=vm,
         scratch_shapes=[
             pltpu.VMEM((TOK, half), BF16),
             pltpu.VMEM((TOK, half), BF16),
             pltpu.VMEM((TOK, half), BF16),
             pltpu.VMEM((half, 2 * half), BF16),
+            pltpu.VMEM((1, HD), jnp.int32),
+            pltpu.VMEM((1, HD), F32),
             pltpu.VMEM((st, 4, CH, HD), F32),
             pltpu.VMEM((st, 4, CH, HD), F32),
             pltpu.VMEM((st, 4, CH, HD), F32),
@@ -406,15 +458,18 @@
             pltpu.VMEM((st, 4, CH, HD), F32),
             pltpu.VMEM((st, 4, CH, HD), F32),
             pltpu.VMEM((HEADS, TOK, HD), F32),
+            pltpu.VMEM((HEADS, TOK, TOK), F32),
+            pltpu.VMEM((HEADS, 6 * HD, 2 * HD), BF16),
+            pltpu.VMEM((HEADS, TOK, 5 * HD), BF16),
             pltpu.VMEM((TOK, half), BF16),
-            pltpu.VMEM((NB, TOK, half // NB), F32),
+            pltpu.VMEM((2 * NB, TOK, half // NB), F32),
             pltpu.VMEM((NB, TOK, half // NB), F32),
             pltpu.VMEM((TOK, TOK), F32),
             pltpu.VMEM((HEADS, HD), F32),
             pltpu.VMEM((40, HD), F32),
             pltpu.VMEM((TOK, HD), F32),
             pltpu.VMEM((TOK, HD), F32),
-            dma((4,)),
+            dma((6,)),
             dma((st, 3)), dma((st, 3)),
             dma((st, 3)), dma((st, 3)),
             dma((st,)), dma((st,)),

time: 39.5 us -> 36.3 us (0.919)
  Pallas kernels: 37.6 us -> 35.2 us
  local copies, waits for them, and re-layouts: 1.67 us -> 0.71 us
    pallas_call x1, Pallas kernels: 37.6 us -> 35.2 us  [on_device(): pl.pallas_call(kernel, out_shape=pltpu.VMEM((TOK, half), BF16), in_specs=...]
    unnamed x1, local copies, waits for them, and re-layouts: 1.67 us -> 0.71 us
where the time goes in v3:
time: 36.3 us; the launch traced here: 35.9 us
  Pallas kernels  35.2 us (97%)
  local copies, waits for them, and re-layouts  0.71 us (2%)
    pallas_call x1, Pallas kernels, on_device(): pl.pallas_call(kernel, out_shape=pltpu.VMEM((TOK, half), BF16), in_specs=...  35.2 us

profile of v3, /device:TPU:225, one launch (start us, length us, event | category | flops | bytes accessed | tf_op | source)
XLA Modules:
  0.0 35.9 jit_solution(16621403320124875391)
XLA Ops:
  0.0 35.2 %mesa.1 = bf16[128,1024]{1,0:T(8,128)(2,1)S(1)} custom-call(bf16[128,1024]{1,0:T(8,128)(2,1)} %q_hbm.1, bf16[128,1024]{1,0:T(8,128)(2,1)} %k_hbm.1, bf16[128,1024]{1,0:T(8,128)(2,1)} %v_hbm.1, s32[1,128]{1,0:T(1,128)} %bitcast.2, f32[1,128]{1,0:T(1,128)} %bitcast.3, bf16[1024,2048]{1,0:T(8,128)(2,1)} %w_hbm.1), custom_call_target="tpu_custom_call" | custom-call | tf_op jit(solution)/shard_map/mesa/pallas_call | solution.py:441
  35.2 0.7 %copy.8 = bf16[128,1024]{1,0:T(8,128)(2,1)} copy(bf16[128,1024]{1,0:T(8,128)(2,1)S(1)} %mesa.1) | data formatting | bytes 524288

commit v4 on v3

--- a/solution.py
+++ b/solution.py
@@ -15,6 +15,8 @@
 ITERS = 4
 CH = 64
 CG = 40
+CROSS = ((0, 1), (2, 3), (4, 5), (6,), (7,))
+STAGES = PAIRS + len(CROSS)
 LAST = 7
 NB = 4
 epsilon = 1e-06
@@ -38,9 +40,9 @@
 def kernel(
     q_hbm, k_hbm, v_hbm, len_hbm, gain_hbm, w_hbm, out_ref,
     q_ref, k_ref, v_ref, w_ref, len_ref, gain_ref,
-    tbuf, ybuf, rbuf, zs, zr, eo, ebuf, qs, scq, rhs, xl, nbuf, acc, other,
+    tbuf, ybuf, rbuf, zs, zr, eo, ebuf, qs, scq, rhs, xl, nbuf, acc, other, obuf,
     mask_ref, ksr, wts, tail_ref, car_ref,
-    lsem, ys, yr, xsd, xr, zsd, zrv, es, er, ps, pr, ready,
+    lsem, ys, yr, xsd, xr, zsd, zrv, es, er, ps, pr, osem, ready,
 ):
     s = lax.axis_index("seq")
     c = lax.axis_index("head")
@@ -127,37 +129,44 @@
         return pl.ds(pl.multiple_of(h * HD, HD), HD)
 
     def rows(st):
-        return pl.ds(0, CG if st < PAIRS else CH)
+        return pl.ds(0, CG if st < PAIRS else 32 * len(CROSS[st - PAIRS]))
+
+    def kind(st):
+        return 0 if st < PAIRS else 1 if len(CROSS[st - PAIRS]) == 2 else 2
 
     def ycopy(st, d):
         r = rows(st)
         return pltpu.make_async_remote_copy(
-            tbuf.at[st, lax.rem(y + d, 4), r], ybuf.at[st, y, r],
-            ys.at[st, d - 1], yr.at[st, d - 1],
+            tbuf.at[st, lax.rem(y + d, 4), r], ybuf.at[st, y, r], ys.at[kind(st)], yr.at[st],
             device_id=(at_y(d), c), device_id_type=MESH,
         )
 
     def xcopy(st, d):
         r = rows(st)
         return pltpu.make_async_remote_copy(
-            rbuf.at[st, x, r], rbuf.at[st, x, r], xsd.at[st, d - 1], xr.at[st, d - 1],
+            rbuf.at[st, x, r], rbuf.at[st, x, r], xsd.at[kind(st)], xr.at[st],
             device_id=(at_x(d), c), device_id_type=MESH,
         )
 
     def zcopy(st):
         r = rows(st)
         return pltpu.make_async_remote_copy(
-            zs.at[st, r], zr.at[st, r], zsd.at[st], zrv.at[st],
+            zs.at[st, r], zr.at[st, r], zsd.at[kind(st)], zrv.at[st],
             device_id=(lax.rem(s + 16, 128), c), device_id_type=MESH,
         )
 
     def ecopy(st, d):
         r = rows(st)
         return pltpu.make_async_remote_copy(
-            eo.at[st, lax.rem(y + d, 4), r], ebuf.at[st, y, r],
-            es.at[st, d - 1], er.at[st, d - 1],
+            eo.at[st, lax.rem(y + d, 4), r], ebuf.at[st, y, r], es.at[kind(st)], er.at[st],
             device_id=(at_y(d), c), device_id_type=MESH,
         )
+
+    def wait_bytes(ref, sem):
+        pltpu.make_async_copy(ref, ref, sem).wait()
+
+    def arrived(ref, sem, st):
+        wait_bytes(ref.at[st, pl.ds(0, 3), rows(st)], sem.at[st])
 
     def send_tail(st):
         r = rows(st)
@@ -193,22 +202,23 @@
         upper = jnp.concatenate([first, second, third, pltpu.roll(second, 96, 1)], 0)
         return jnp.where(ci // 32 >= ri // 32, upper, upper.T)
 
-    def cross_stage(g):
-        for i in range(2):
-            h = 2 * g + i
+    def cross_stage(st):
+        parts = []
+        for h in CROSS[st - PAIRS]:
             k = k_ref[:, head_cols(h)]
             v = v_ref[:, head_cols(h)]
             kf = k.astype(F32)
             ks = lax.rsqrt(jnp.sum(kf * kf, axis=1, keepdims=True) + epsilon)
             hi, lo = split2(kf * ks * tail_ref[...])
-            cross = dot(jnp.concatenate([hi, lo], 0), jnp.concatenate([v, v], 0), TN)
-            tbuf[PAIRS + g, 2 * i] = cross[:CH]
-            tbuf[PAIRS + g, 2 * i + 1] = cross[CH:]
+            parts.append(dot(jnp.concatenate([hi, lo], 0), jnp.concatenate([v, v], 0), TN))
+        n = 32 * len(parts)
+        stacked = jnp.concatenate(parts, 0)
+        for o in range(4):
+            tbuf[st, o, :n] = stacked[n * o : n * (o + 1)]
 
     def row_sum(st):
         r = rows(st)
-        for d in (1, 2, 3):
-            ycopy(st, d).wait_recv()
+        arrived(ybuf, yr, st)
         total = ybuf[st, 3, r]
         for i in range(3):
             total = total + wt(WR + i) * ybuf[st, i, r]
@@ -218,8 +228,7 @@
 
     def plane_sum(st):
         r = rows(st)
-        for d in (1, 2, 3):
-            xcopy(st, d).wait_recv()
+        arrived(rbuf, xr, st)
         total = rbuf[st, 3, r]
         for i in range(3):
             total = total + wt(WZ + i) * rbuf[st, i, r]
@@ -266,12 +275,12 @@
             rhs[h, 4 * HD : 5 * HD] = both
             rhs[h, 5 * HD :] = jnp.concatenate([jnp.zeros_like(klo), klo], 1)
 
-    def solve(g):
-        for d in (1, 2, 3):
-            ecopy(g, d).wait_recv()
+    def solve(pairs):
         car16 = car_ref[...].astype(BF16)
         state = []
-        for i in range(2):
+        for g, i in [(g, i) for g in pairs for i in range(2)]:
+            if i == 0:
+                arrived(ebuf, er, g)
             h = 2 * g + i
             k = k_ref[:, head_cols(h)]
             ghi, glo = split2(gram_of(g, i))
@@ -312,6 +321,7 @@
                     e["p"] = e["r"] + beta * p
                     e["sp"] = e["sr"] + beta * sp
                     e["n"] = new
+            yield
         for e in state:
             h = e["h"]
             hi, lo = split2(e["x"])
@@ -319,15 +329,13 @@
             chi = hi * car16
             xl[h] = jnp.concatenate([chi, lo * car16, chi, shi, slo], 1)
 
-    def finish(g):
-        st = PAIRS + g
-        for d in (1, 2, 3):
-            ecopy(st, d).wait_recv()
-        for i in range(2):
-            h = 2 * g + i
+    def finish(st):
+        arrived(ebuf, er, st)
+        n = 32 * len(CROSS[st - PAIRS])
+        stacked = jnp.concatenate([ebuf[st, o, :n] for o in range(4)], 0)
+        for i, h in enumerate(CROSS[st - PAIRS]):
             v = v_ref[:, head_cols(h)]
-            cross = jnp.concatenate([ebuf[st, 2 * i], ebuf[st, 2 * i + 1]], 0)
-            xhi, xlo = split2(cross)
+            xhi, xlo = split2(stacked[HD * i : HD * (i + 1)])
             mixed = dot(xl[h], jnp.concatenate([xhi, xhi, xlo, v, v], 0), NN)
             inv = lax.rsqrt(jnp.sum(mixed * mixed, axis=1, keepdims=True) / HD + epsilon)
             nbuf[:, head_cols(h)] = (mixed * inv * gain_ref[...]).astype(BF16)
@@ -360,54 +368,67 @@
         gram_stage(g)
         send_tail(g)
     VAL.wait()
-    for g in range(PAIRS):
-        cross_stage(g)
-        send_tail(PAIRS + g)
+    for st in range(PAIRS, STAGES):
+        cross_stage(st)
+        send_tail(st)
     row_sum(0)
     row_sum(1)
     QUERY.wait()
     prepare(0)
     row_sum(2)
     row_sum(3)
+    prepare(1)
+    row_sum(4)
     plane_sum(0)
-    prepare(1)
     plane_sum(1)
-    row_sum(4)
+    row_sum(5)
     plane_sum(2)
     give_back(0)
     plane_sum(3)
-    row_sum(5)
+    row_sum(6)
     give_back(1)
     prepare(2)
-    row_sum(6)
+    row_sum(7)
     give_back(2)
+    row_sum(8)
     plane_sum(4)
+    prepare(3)
     give_back(3)
-    prepare(3)
-    row_sum(7)
     plane_sum(5)
     give_back(4)
-    solve(0)
+    first = solve((0, 1))
+    next(first)
     plane_sum(6)
     give_back(5)
+    next(first)
     plane_sum(7)
-    solve(1)
+    plane_sum(8)
+    next(first)
     give_back(6)
+    next(first)
     give_back(7)
-    solve(2)
-    solve(3)
+    give_back(8)
+    for _ in first:
+        pass
+    for _ in solve((2, 3)):
+        pass
     GAIN.wait()
     WEIGHT.wait()
     for g in range(PAIRS - 1):
-        finish(g)
+        finish(PAIRS + g)
         project_pair(g)
-    finish(PAIRS - 1)
+    finish(7)
+    finish(8)
 
     def pcopy(b):
         return pltpu.make_async_remote_copy(
-            acc.at[b], other.at[b], ps.at[b], pr.at[b],
+            acc.at[b], other.at[b], ps.at[0], pr.at[b],
             device_id=(s, 1 - c), device_id_type=MESH,
         )
+
+    def ocopy(b):
+        part = (slice(None), pl.ds(b * width, width))
+        return pltpu.make_async_copy(obuf.at[part], out_ref.at[part], osem.at[0])
 
     for b in range(NB):
         acc[b] = acc[b] + project(PAIRS - 1, b)
@@ -415,34 +436,33 @@
     for b in range(NB):
         mine = acc[NB + b] + project(PAIRS - 1, NB + b)
         pcopy(b).wait_recv()
-        out_ref[:, b * width : (b + 1) * width] = (mine + other[b]).astype(BF16)
-
-    for st in range(2 * PAIRS):
-        for d in (1, 2, 3):
-            ycopy(st, d).wait_send()
-            xcopy(st, d).wait_send()
-            ecopy(st, d).wait_send()
-
-    @pl.when(z < LAST)
-    def _():
-        for st in range(2 * PAIRS):
-            zcopy(st).wait_send()
-
-    for b in range(NB):
-        pcopy(b).wait_send()
+        obuf[:, b * width : (b + 1) * width] = (mine + other[b]).astype(BF16)
+        ocopy(b).start()
+
+    for i in range(3):
+        group = [st for st in range(STAGES) if kind(st) == i]
+        several = pl.ds(group[0], len(group))
+        for ref, sem in ((ybuf, ys), (rbuf, xsd), (ebuf, es)):
+            wait_bytes(ref.at[several, pl.ds(0, 3), rows(group[0])], sem.at[i])
+
+        @pl.when(z < LAST)
+        def _():
+            wait_bytes(zs.at[several, rows(group[0])], zsd.at[i])
+
+    wait_bytes(other, ps.at[0])
+    wait_bytes(obuf, osem.at[0])
 
 
 def on_device(query_rows, key_rows, value_rows, doc_lengths, norm_gain, out_weight):
     half = HEADS * HD
-    st = 2 * PAIRS
+    st = STAGES
     dma = pltpu.SemaphoreType.DMA
-    vm = pl.BlockSpec(memory_space=pltpu.VMEM)
     anywhere = pl.BlockSpec(memory_space=pl.ANY)
     return pl.pallas_call(
         kernel,
         out_shape=pltpu.VMEM((TOK, half), BF16),
         in_specs=[anywhere] * 6,
-        out_specs=vm,
+        out_specs=anywhere,
         scratch_shapes=[
             pltpu.VMEM((TOK, half), BF16),
             pltpu.VMEM((TOK, half), BF16),
@@ -464,17 +484,18 @@
             pltpu.VMEM((TOK, half), BF16),
             pltpu.VMEM((2 * NB, TOK, half // NB), F32),
             pltpu.VMEM((NB, TOK, half // NB), F32),
+            pltpu.VMEM((TOK, half), BF16),
             pltpu.VMEM((TOK, TOK), F32),
             pltpu.VMEM((HEADS, HD), F32),
             pltpu.VMEM((40, HD), F32),
             pltpu.VMEM((TOK, HD), F32),
             pltpu.VMEM((TOK, HD), F32),
             dma((6,)),
-            dma((st, 3)), dma((st, 3)),
-            dma((st, 3)), dma((st, 3)),
-            dma((st,)), dma((st,)),
-            dma((st, 3)), dma((st, 3)),
-            dma((NB,)), dma((NB,)),
+            dma((3,)), dma((st,)),
+            dma((3,)), dma((st,)),
+            dma((3,)), dma((st,)),
+            dma((3,)), dma((st,)),
+            dma((1,)), dma((NB,)), dma((1,)),
             pltpu.SemaphoreType.REGULAR,
         ],
         compiler_params=pltpu.CompilerParams(collective_id=0, has_side_effects=True),

time: 36.3 us -> 33.4 us (0.920); the launches traced: 35.9 us -> 33.4 us
  Pallas kernels: 35.2 us -> 32.7 us
    pallas_call x1, Pallas kernels: 35.2 us -> 32.7 us  [on_device(): pl.pallas_call(kernel, out_shape=pltpu.VMEM((TOK, half), BF16), in_specs=...]
where the time goes in v4:
time: 33.4 us
  Pallas kernels  32.7 us (98%)
  local copies, waits for them, and re-layouts  0.71 us (2%)
    pallas_call x1, Pallas kernels, on_device(): pl.pallas_call(kernel, out_shape=pltpu.VMEM((TOK, half), BF16), in_specs=...  32.7 us
    unnamed x1, local copies, waits for them, and re-layouts  0.71 us

profile of v4, /device:TPU:225, one launch (start us, length us, event | category | flops | bytes accessed | tf_op | source)
XLA Modules:
  0.0 33.4 jit_solution(14208946456066366377)
XLA Ops:
  0.0 32.7 %mesa.1 = bf16[128,1024]{1,0:T(8,128)(2,1)S(1)} custom-call(bf16[128,1024]{1,0:T(8,128)(2,1)} %q_hbm.1, bf16[128,1024]{1,0:T(8,128)(2,1)} %k_hbm.1, bf16[128,1024]{1,0:T(8,128)(2,1)} %v_hbm.1, s32[1,128]{1,0:T(1,128)} %bitcast.2, f32[1,128]{1,0:T(1,128)} %bitcast.3, bf16[1024,2048]{1,0:T(8,128)(2,1)} %w_hbm.1), custom_call_target="tpu_custom_call" | custom-call | tf_op jit(solution)/shard_map/mesa/pallas_call | solution.py:461
  32.7 0.7 %copy.8 = bf16[128,1024]{1,0:T(8,128)(2,1)} copy(bf16[128,1024]{1,0:T(8,128)(2,1)S(1)} %mesa.1) | data formatting | bytes 524288

commit v5 on v4

--- a/solution.py
+++ b/solution.py
@@ -40,9 +40,9 @@
 def kernel(
     q_hbm, k_hbm, v_hbm, len_hbm, gain_hbm, w_hbm, out_ref,
     q_ref, k_ref, v_ref, w_ref, len_ref, gain_ref,
-    tbuf, ybuf, rbuf, zs, zr, eo, ebuf, qs, scq, rhs, xl, nbuf, acc, other, obuf,
-    mask_ref, ksr, wts, tail_ref, car_ref,
-    lsem, ys, yr, xsd, xr, zsd, zrv, es, er, ps, pr, osem, ready,
+    tbuf, ybuf, rbuf, zs, zr, eo, ebuf, qs, scq, lhs, xl, vt, mf, mg, nbuf, acc, other, obuf,
+    mask_ref, wts, tail_ref, car_ref,
+    lsem, sent, yr, xr, zsd, zrv, er, ps, pr, osem, ready,
 ):
     s = lax.axis_index("seq")
     c = lax.axis_index("head")
@@ -106,9 +106,9 @@
         wts[k : k + 1, :] = jnp.broadcast_to(jnp.where(flag, 1.0, 0.0), (1, HD))
 
     here, before = end_of(s), end_of(s - 1)
-    car_ref[...] = jnp.broadcast_to(jnp.where(doc_col == before, 1.0, 0.0), (TOK, HD))
+    car_ref[...] = jnp.where(doc_row == before, 1.0, 0.0)
     tail_ref[...] = jnp.broadcast_to(jnp.where(doc_col == here, 1.0, 0.0), (TOK, HD))
-    mask_ref[...] = jnp.where((doc_col == doc_row) & (ci <= ri), 1.0, 0.0)
+    mask_ref[...] = jnp.where((doc_col == doc_row) & (ri <= ci), 1.0, 0.0)
     dy = [end_of(row + i) for i in range(4)]
     dx = [end_of(16 * z + 4 * i + 3) for i in range(4)]
     dprev, dplane = end_of(row - 1), end_of(16 * z - 1)
@@ -137,14 +137,14 @@
     def ycopy(st, d):
         r = rows(st)
         return pltpu.make_async_remote_copy(
-            tbuf.at[st, lax.rem(y + d, 4), r], ybuf.at[st, y, r], ys.at[kind(st)], yr.at[st],
+            tbuf.at[st, lax.rem(y + d, 4), r], ybuf.at[st, y, r], sent.at[kind(st)], yr.at[st],
             device_id=(at_y(d), c), device_id_type=MESH,
         )
 
     def xcopy(st, d):
         r = rows(st)
         return pltpu.make_async_remote_copy(
-            rbuf.at[st, x, r], rbuf.at[st, x, r], xsd.at[kind(st)], xr.at[st],
+            rbuf.at[st, x, r], rbuf.at[st, x, r], sent.at[kind(st)], xr.at[st],
             device_id=(at_x(d), c), device_id_type=MESH,
         )
 
@@ -158,7 +158,7 @@
     def ecopy(st, d):
         r = rows(st)
         return pltpu.make_async_remote_copy(
-            eo.at[st, lax.rem(y + d, 4), r], ebuf.at[st, y, r], es.at[kind(st)], er.at[st],
+            eo.at[st, lax.rem(y + d, 4), r], ebuf.at[st, y, r], sent.at[kind(st)], er.at[st],
             device_id=(at_y(d), c), device_id_type=MESH,
         )
 
@@ -182,7 +182,6 @@
             k = k_ref[:, head_cols(h)]
             kf = k.astype(F32)
             ks = lax.rsqrt(jnp.sum(kf * kf, axis=1, keepdims=True) + epsilon)
-            ksr[h : h + 1, :] = jnp.sum(jnp.where(ri == ci, ks, 0.0), axis=0, keepdims=True)
             hi, lo = split2(kf * (ks * ks) * tail_ref[...])
             grams.append(dot(jnp.concatenate([hi, lo], 0), jnp.concatenate([k, k], 0), TN))
         blocks = []
@@ -210,7 +209,7 @@
             kf = k.astype(F32)
             ks = lax.rsqrt(jnp.sum(kf * kf, axis=1, keepdims=True) + epsilon)
             hi, lo = split2(kf * ks * tail_ref[...])
-            parts.append(dot(jnp.concatenate([hi, lo], 0), jnp.concatenate([v, v], 0), TN))
+            parts.append(dot(jnp.concatenate([v, v], 0), jnp.concatenate([hi, lo], 0), TN))
         n = 32 * len(parts)
         stacked = jnp.concatenate(parts, 0)
         for o in range(4):
@@ -263,20 +262,31 @@
 
     def prepare(g):
         for h in (2 * g, 2 * g + 1):
-            q = q_ref[:, head_cols(h)].astype(F32)
-            qn = q * lax.rsqrt(jnp.sum(q * q, axis=1, keepdims=True) + epsilon)
+            q = q_ref[:, head_cols(h)].astype(F32).T
+            q = q * lax.rsqrt(jnp.sum(q * q, axis=0, keepdims=True) + epsilon)
             k = k_ref[:, head_cols(h)]
-            hi, lo = split2(qn)
-            qs[h] = qn
-            scq[h] = dot(jnp.concatenate([hi, lo], 1), jnp.concatenate([k, k], 1), NT)
+            kf = k.astype(F32)
+            ks = lax.rsqrt(jnp.sum(kf * kf, axis=1, keepdims=True) + epsilon)
+            m = mask_ref[...] * ks
+            mf[h] = m
+            mg[h] = m * ks
+            hi, lo = split2(q)
+            qs[h] = q
+            scq[h] = dot(jnp.concatenate([k, k], 1), jnp.concatenate([hi, lo], 0), NN)
             khi, klo = split2(dot(k, k, NT))
-            both = jnp.concatenate([k, khi], 1)
-            rhs[h, 3 * HD : 4 * HD] = both
-            rhs[h, 4 * HD : 5 * HD] = both
-            rhs[h, 5 * HD :] = jnp.concatenate([jnp.zeros_like(klo), klo], 1)
+            lhs[h, :HD, HD : 2 * HD] = kf.T.astype(BF16)
+            lhs[h, HD:, HD : 2 * HD] = khi
+            lhs[h, :HD, 3 * HD :] = jnp.zeros_like(klo)
+            lhs[h, HD:, 3 * HD :] = klo
+            vt[h] = v_ref[:, head_cols(h)].astype(F32).T.astype(BF16)
+
+    def columns_of(vector, scores):
+        hi, lo = split2(vector)
+        shi, slo = split2(scores)
+        car16 = car_ref[...].astype(BF16)
+        return jnp.concatenate([hi * car16, shi], 0), jnp.concatenate([lo * car16, slo], 0)
 
     def solve(pairs):
-        car16 = car_ref[...].astype(BF16)
         state = []
         for g, i in [(g, i) for g in pairs for i in range(2)]:
             if i == 0:
@@ -284,39 +294,32 @@
             h = 2 * g + i
             k = k_ref[:, head_cols(h)]
             ghi, glo = split2(gram_of(g, i))
-            shi, slo = split2(dot(jnp.concatenate([ghi, glo], 1), jnp.concatenate([k, k], 1), NT))
-            both = jnp.concatenate([ghi, shi], 1)
-            rhs[h, :HD] = both
-            rhs[h, HD : 2 * HD] = both
-            rhs[h, 2 * HD : 3 * HD] = jnp.concatenate([glo, slo], 1)
-            ksrow = ksr[h : h + 1, :]
-            qn, sc = qs[h], scq[h]
-            state.append(
-                dict(
-                    h=h, m=mask_ref[...] * (ksrow * ksrow), p=qn, sp=sc, r=qn, sr=sc,
-                    n=jnp.sum(qn * qn, axis=1, keepdims=True),
-                )
-            )
+            shi, slo = split2(dot(jnp.concatenate([k, k], 1), jnp.concatenate([ghi, glo], 0), NN))
+            lhs[h, :HD, :HD] = ghi
+            lhs[h, HD:, :HD] = shi
+            lhs[h, :HD, 2 * HD : 3 * HD] = glo
+            lhs[h, HD:, 2 * HD : 3 * HD] = slo
+            q, sc = qs[h], scq[h]
+            n = jnp.sum(q * q, axis=0, keepdims=True)
+            state.append(dict(h=h, p=q, sp=sc, r=q, sr=sc, n=n))
+        yield
         for it in range(ITERS):
             last = it == ITERS - 1
+            rows_here = HD if last else 2 * HD
             for e in state:
-                p, sp = e["p"], e["sp"]
-                hi, lo = split2(p)
-                shi, slo = split2(sp * e["m"])
-                chi = hi * car16
-                lhs = jnp.concatenate([chi, lo * car16, chi, shi, slo, shi], 1)
-                if last:
-                    a = dot(lhs[:, : 5 * HD], rhs[e["h"], : 5 * HD, :HD], NN) + damping * p
-                else:
-                    both = dot(lhs, rhs[e["h"]], NN)
-                    a, sa = both[:, :HD] + damping * p, both[:, HD:] + damping * sp
-                alpha = e["n"] / (jnp.sum(p * a, axis=1, keepdims=True) + epsilon)
+                p, sp, h = e["p"], e["sp"], e["h"]
+                hi, lo = columns_of(p, sp * mg[h])
+                both = dot(lhs[h, :rows_here, : 2 * HD], jnp.concatenate([hi, lo], 1), NN)
+                both = both[:, :TOK] + both[:, TOK:] + dot(lhs[h, :rows_here, 2 * HD :], hi, NN)
+                a = both[:HD] + damping * p
+                alpha = e["n"] / (jnp.sum(p * a, axis=0, keepdims=True) + epsilon)
                 e["x"] = alpha * p if it == 0 else e["x"] + alpha * p
                 e["sx"] = alpha * sp if it == 0 else e["sx"] + alpha * sp
                 if not last:
+                    sa = both[HD:] + damping * sp
                     e["r"] = e["r"] - alpha * a
                     e["sr"] = e["sr"] - alpha * sa
-                    new = jnp.sum(e["r"] * e["r"], axis=1, keepdims=True)
+                    new = jnp.sum(e["r"] * e["r"], axis=0, keepdims=True)
                     beta = new / (e["n"] + epsilon)
                     e["p"] = e["r"] + beta * p
                     e["sp"] = e["sr"] + beta * sp
@@ -324,21 +327,27 @@
             yield
         for e in state:
             h = e["h"]
-            hi, lo = split2(e["x"])
-            shi, slo = split2(e["sx"] * (mask_ref[...] * ksr[h : h + 1, :]))
-            chi = hi * car16
-            xl[h] = jnp.concatenate([chi, lo * car16, chi, shi, slo], 1)
-
-    def finish(st):
-        arrived(ebuf, er, st)
-        n = 32 * len(CROSS[st - PAIRS])
-        stacked = jnp.concatenate([ebuf[st, o, :n] for o in range(4)], 0)
-        for i, h in enumerate(CROSS[st - PAIRS]):
-            v = v_ref[:, head_cols(h)]
-            xhi, xlo = split2(stacked[HD * i : HD * (i + 1)])
-            mixed = dot(xl[h], jnp.concatenate([xhi, xhi, xlo, v, v], 0), NN)
-            inv = lax.rsqrt(jnp.sum(mixed * mixed, axis=1, keepdims=True) / HD + epsilon)
-            nbuf[:, head_cols(h)] = (mixed * inv * gain_ref[...]).astype(BF16)
+            hi, lo = columns_of(e["x"], e["sx"] * mf[h])
+            xl[h] = jnp.concatenate([hi, lo], 1)
+
+    def finish(*stages):
+        for st in stages:
+            arrived(ebuf, er, st)
+        states = []
+        for st in stages:
+            n = 32 * len(CROSS[st - PAIRS])
+            stacked = jnp.concatenate([ebuf[st, o, :n] for o in range(4)], 0)
+            for i, h in enumerate(CROSS[st - PAIRS]):
+                states.append((h, stacked[HD * i : HD * (i + 1)]))
+        for h, cross in states:
+            xhi, xlo = split2(cross)
+            mixed = dot(jnp.concatenate([xhi, vt[h]], 1), xl[h], NN)
+            mixed = mixed[:, :TOK] + mixed[:, TOK:] + dot(xlo, xl[h, :HD, :TOK], NN)
+            inv = lax.rsqrt(jnp.sum(mixed * mixed, axis=0, keepdims=True) / HD + epsilon)
+            nbuf[:, head_cols(h)] = (mixed * inv * gain_col()).T.astype(BF16)
+
+    def gain_col():
+        return jnp.sum(jnp.where(ri == ci, gain_ref[...], 0.0), axis=1, keepdims=True)
 
     half = HEADS * HD
     width = half // NB
@@ -396,29 +405,30 @@
     give_back(3)
     plane_sum(5)
     give_back(4)
+    plane_sum(6)
     first = solve((0, 1))
     next(first)
-    plane_sum(6)
+    next(first)
     give_back(5)
-    next(first)
     plane_sum(7)
     plane_sum(8)
     next(first)
+    next(first)
     give_back(6)
-    next(first)
+    for _ in first:
+        pass
+    second = solve((2, 3))
+    next(second)
     give_back(7)
     give_back(8)
-    for _ in first:
-        pass
-    for _ in solve((2, 3)):
+    for _ in second:
         pass
     GAIN.wait()
     WEIGHT.wait()
     for g in range(PAIRS - 1):
         finish(PAIRS + g)
         project_pair(g)
-    finish(7)
-    finish(8)
+    finish(7, 8)
 
     def pcopy(b):
         return pltpu.make_async_remote_copy(
@@ -430,24 +440,25 @@
         part = (slice(None), pl.ds(b * width, width))
         return pltpu.make_async_copy(obuf.at[part], out_ref.at[part], osem.at[0])
 
+    for b in range(0, NB, 2):
+        for e in (b, b + 1):
+            acc[e] = acc[e] + project(PAIRS - 1, e)
+        for e in (b, b + 1):
+            pcopy(e).start()
+    for b in range(NB, 2 * NB):
+        acc[b] = acc[b] + project(PAIRS - 1, b)
     for b in range(NB):
-        acc[b] = acc[b] + project(PAIRS - 1, b)
-        pcopy(b).start()
-    for b in range(NB):
-        mine = acc[NB + b] + project(PAIRS - 1, NB + b)
         pcopy(b).wait_recv()
-        obuf[:, b * width : (b + 1) * width] = (mine + other[b]).astype(BF16)
+        obuf[:, b * width : (b + 1) * width] = (acc[NB + b] + other[b]).astype(BF16)
         ocopy(b).start()
 
-    for i in range(3):
+    for i, (stages, slots) in enumerate(((9, 4), (9, 3), (6, 3))):
         group = [st for st in range(STAGES) if kind(st) == i]
-        several = pl.ds(group[0], len(group))
-        for ref, sem in ((ybuf, ys), (rbuf, xsd), (ebuf, es)):
-            wait_bytes(ref.at[several, pl.ds(0, 3), rows(group[0])], sem.at[i])
+        wait_bytes(ybuf.at[pl.ds(0, stages), pl.ds(0, slots), rows(group[0])], sent.at[i])
 
         @pl.when(z < LAST)
         def _():
-            wait_bytes(zs.at[several, rows(group[0])], zsd.at[i])
+            wait_bytes(zs.at[pl.ds(group[0], len(group)), rows(group[0])], zsd.at[i])
 
     wait_bytes(other, ps.at[0])
     wait_bytes(obuf, osem.at[0])
@@ -479,22 +490,22 @@
             pltpu.VMEM((st, 4, CH, HD), F32),
             pltpu.VMEM((HEADS, TOK, HD), F32),
             pltpu.VMEM((HEADS, TOK, TOK), F32),
-            pltpu.VMEM((HEADS, 6 * HD, 2 * HD), BF16),
-            pltpu.VMEM((HEADS, TOK, 5 * HD), BF16),
+            pltpu.VMEM((HEADS, 2 * HD, 4 * HD), BF16),
+            pltpu.VMEM((HEADS, 2 * HD, 2 * TOK), BF16),
+            pltpu.VMEM((HEADS, HD, TOK), BF16),
+            pltpu.VMEM((HEADS, TOK, TOK), F32),
+            pltpu.VMEM((HEADS, TOK, TOK), F32),
             pltpu.VMEM((TOK, half), BF16),
             pltpu.VMEM((2 * NB, TOK, half // NB), F32),
             pltpu.VMEM((NB, TOK, half // NB), F32),
             pltpu.VMEM((TOK, half), BF16),
             pltpu.VMEM((TOK, TOK), F32),
-            pltpu.VMEM((HEADS, HD), F32),
             pltpu.VMEM((40, HD), F32),
             pltpu.VMEM((TOK, HD), F32),
-            pltpu.VMEM((TOK, HD), F32),
+            pltpu.VMEM((1, TOK), F32),
             dma((6,)),
-            dma((3,)), dma((st,)),
-            dma((3,)), dma((st,)),
-            dma((3,)), dma((st,)),
-            dma((3,)), dma((st,)),
+            dma((3,)), dma((st,)), dma((st,)),
+            dma((3,)), dma((st,)), dma((st,)),
             dma((1,)), dma((NB,)), dma((1,)),
             pltpu.SemaphoreType.REGULAR,
         ],

time: 33.4 us -> 32.5 us (0.973)
  Pallas kernels: 32.7 us -> 31.7 us
    pallas_call x1, Pallas kernels: 32.7 us -> 31.7 us  [on_device(): pl.pallas_call(kernel, out_shape=pltpu.VMEM((TOK, half), BF16), in_specs=...]
where the time goes in v5:
time: 32.5 us; the launch traced here: 32.4 us
  Pallas kernels  31.7 us (98%)
  local copies, waits for them, and re-layouts  0.71 us (2%)
    pallas_call x1, Pallas kernels, on_device(): pl.pallas_call(kernel, out_shape=pltpu.VMEM((TOK, half), BF16), in_specs=...  31.7 us
    unnamed x1, local copies, waits for them, and re-layouts  0.71 us

profile of v5, /device:TPU:225, one launch (start us, length us, event | category | flops | bytes accessed | tf_op | source)
XLA Modules:
  0.0 32.4 jit_solution(4543966500914806682)
XLA Ops:
  0.0 31.7 %mesa.1 = bf16[128,1024]{1,0:T(8,128)(2,1)S(1)} custom-call(bf16[128,1024]{1,0:T(8,128)(2,1)} %q_hbm.1, bf16[128,1024]{1,0:T(8,128)(2,1)} %k_hbm.1, bf16[128,1024]{1,0:T(8,128)(2,1)} %v_hbm.1, s32[1,128]{1,0:T(1,128)} %bitcast.2, f32[1,128]{1,0:T(1,128)} %bitcast.3, bf16[1024,2048]{1,0:T(8,128)(2,1)} %w_hbm.1), custom_call_target="tpu_custom_call" | custom-call | tf_op jit(solution)/shard_map/mesa/pallas_call | solution.py:472
  31.7 0.7 %copy.8 = bf16[128,1024]{1,0:T(8,128)(2,1)} copy(bf16[128,1024]{1,0:T(8,128)(2,1)S(1)} %mesa.1) | data formatting | bytes 524288

commit v6 on v5

--- a/solution.py
+++ b/solution.py
@@ -40,9 +40,9 @@
 def kernel(
     q_hbm, k_hbm, v_hbm, len_hbm, gain_hbm, w_hbm, out_ref,
     q_ref, k_ref, v_ref, w_ref, len_ref, gain_ref,
-    tbuf, ybuf, rbuf, zs, zr, eo, ebuf, qs, scq, lhs, xl, vt, mf, mg, nbuf, acc, other, obuf,
+    tbuf, ybuf, rbuf, zs, zr, eo, ebuf, qs, scq, lhs, xl, vt, mf, mg, nbuf, acc, other,
     mask_ref, wts, tail_ref, car_ref,
-    lsem, sent, yr, xr, zsd, zrv, er, ps, pr, osem, ready,
+    lsem, sent, yr, xr, zsd, zrv, er, ps, pr, ready,
 ):
     s = lax.axis_index("seq")
     c = lax.axis_index("head")
@@ -170,7 +170,7 @@
 
     def send_tail(st):
         r = rows(st)
-        for d in (1, 2, 3):
+        for d in (2, 1, 3):
             ycopy(st, d).start()
         ybuf[st, y, r] = tbuf[st, y, r]
 
@@ -222,7 +222,7 @@
         for i in range(3):
             total = total + wt(WR + i) * ybuf[st, i, r]
         rbuf[st, x, r] = total
-        for d in (1, 2, 3):
+        for d in (2, 1, 3):
             xcopy(st, d).start()
 
     def plane_sum(st):
@@ -256,7 +256,7 @@
             for i in range(t):
                 total = total + wt(WE + 4 * t + i) * parts[i]
             eo[st, t, r] = total
-        for d in (1, 2, 3):
+        for d in (2, 1, 3):
             ecopy(st, d).start()
         ebuf[st, y, r] = eo[st, y, r]
 
@@ -377,15 +377,30 @@
         gram_stage(g)
         send_tail(g)
     VAL.wait()
+    def send_early(st):
+        @pl.when(c == 0)
+        def _():
+            send_tail(st)
+
+    def send_late(st):
+        @pl.when(c == 1)
+        def _():
+            send_tail(st)
+
     for st in range(PAIRS, STAGES):
         cross_stage(st)
-        send_tail(st)
+        send_early(st)
     row_sum(0)
+    send_late(4)
     row_sum(1)
+    send_late(5)
     QUERY.wait()
     prepare(0)
     row_sum(2)
+    send_late(6)
     row_sum(3)
+    send_late(7)
+    send_late(8)
     prepare(1)
     row_sum(4)
     plane_sum(0)
@@ -404,8 +419,8 @@
     prepare(3)
     give_back(3)
     plane_sum(5)
+    plane_sum(6)
     give_back(4)
-    plane_sum(6)
     first = solve((0, 1))
     next(first)
     next(first)
@@ -425,9 +440,11 @@
         pass
     GAIN.wait()
     WEIGHT.wait()
-    for g in range(PAIRS - 1):
-        finish(PAIRS + g)
-        project_pair(g)
+    finish(4, 5)
+    project_pair(0)
+    project_pair(1)
+    finish(6)
+    project_pair(2)
     finish(7, 8)
 
     def pcopy(b):
@@ -435,10 +452,6 @@
             acc.at[b], other.at[b], ps.at[0], pr.at[b],
             device_id=(s, 1 - c), device_id_type=MESH,
         )
-
-    def ocopy(b):
-        part = (slice(None), pl.ds(b * width, width))
-        return pltpu.make_async_copy(obuf.at[part], out_ref.at[part], osem.at[0])
 
     for b in range(0, NB, 2):
         for e in (b, b + 1):
@@ -449,8 +462,7 @@
         acc[b] = acc[b] + project(PAIRS - 1, b)
     for b in range(NB):
         pcopy(b).wait_recv()
-        obuf[:, b * width : (b + 1) * width] = (acc[NB + b] + other[b]).astype(BF16)
-        ocopy(b).start()
+        out_ref[:, b * width : (b + 1) * width] = (acc[NB + b] + other[b]).astype(BF16)
 
     for i, (stages, slots) in enumerate(((9, 4), (9, 3), (6, 3))):
         group = [st for st in range(STAGES) if kind(st) == i]
@@ -461,7 +473,6 @@
             wait_bytes(zs.at[pl.ds(group[0], len(group)), rows(group[0])], zsd.at[i])
 
     wait_bytes(other, ps.at[0])
-    wait_bytes(obuf, osem.at[0])
 
 
 def on_device(query_rows, key_rows, value_rows, doc_lengths, norm_gain, out_weight):
@@ -473,7 +484,7 @@
         kernel,
         out_shape=pltpu.VMEM((TOK, half), BF16),
         in_specs=[anywhere] * 6,
-        out_specs=anywhere,
+        out_specs=pl.BlockSpec(memory_space=pltpu.VMEM),
         scratch_shapes=[
             pltpu.VMEM((TOK, half), BF16),
             pltpu.VMEM((TOK, half), BF16),
@@ -498,7 +509,6 @@
             pltpu.VMEM((TOK, half), BF16),
             pltpu.VMEM((2 * NB, TOK, half // NB), F32),
             pltpu.VMEM((NB, TOK, half // NB), F32),
-            pltpu.VMEM((TOK, half), BF16),
             pltpu.VMEM((TOK, TOK), F32),
             pltpu.VMEM((40, HD), F32),
             pltpu.VMEM((TOK, HD), F32),
@@ -506,7 +516,7 @@
             dma((6,)),
             dma((3,)), dma((st,)), dma((st,)),
             dma((3,)), dma((st,)), dma((st,)),
-            dma((1,)), dma((NB,)), dma((1,)),
+            dma((1,)), dma((NB,)),
             pltpu.SemaphoreType.REGULAR,
         ],
         compiler_params=pltpu.CompilerParams(collective_id=0, has_side_effects=True),

time: 32.5 us -> 31.5 us (0.969)
  Pallas kernels: 31.7 us -> 30.7 us
    pallas_call x1, Pallas kernels: 31.7 us -> 30.7 us  [on_device(): pl.pallas_call(kernel, out_shape=pltpu.VMEM((TOK, half), BF16), in_specs=...]
where the time goes in v6:
time: 31.5 us; the launch traced here: 31.4 us
  Pallas kernels  30.7 us (97%)
  local copies, waits for them, and re-layouts  0.71 us (2%)
    pallas_call x1, Pallas kernels, on_device(): pl.pallas_call(kernel, out_shape=pltpu.VMEM((TOK, half), BF16), in_specs=...  30.7 us
    unnamed x1, local copies, waits for them, and re-layouts  0.71 us

profile of v6, /device:TPU:225, one launch (start us, length us, event | category | flops | bytes accessed | tf_op | source)
XLA Modules:
  0.0 31.4 jit_solution(7522564039376785004)
XLA Ops:
  0.0 30.7 %mesa.1 = bf16[128,1024]{1,0:T(8,128)(2,1)S(1)} custom-call(bf16[128,1024]{1,0:T(8,128)(2,1)} %q_hbm.1, bf16[128,1024]{1,0:T(8,128)(2,1)} %k_hbm.1, bf16[128,1024]{1,0:T(8,128)(2,1)} %v_hbm.1, s32[1,128]{1,0:T(1,128)} %bitcast.2, f32[1,128]{1,0:T(1,128)} %bitcast.3, bf16[1024,2048]{1,0:T(8,128)(2,1)} %w_hbm.1), custom_call_target="tpu_custom_call" | custom-call | tf_op jit(solution)/shard_map/mesa/pallas_call | solution.py:483
  30.7 0.7 %copy.8 = bf16[128,1024]{1,0:T(8,128)(2,1)} copy(bf16[128,1024]{1,0:T(8,128)(2,1)S(1)} %mesa.1) | data formatting | bytes 524288

commit v7 on v6

--- a/solution.py
+++ b/solution.py
@@ -302,7 +302,8 @@
             q, sc = qs[h], scq[h]
             n = jnp.sum(q * q, axis=0, keepdims=True)
             state.append(dict(h=h, p=q, sp=sc, r=q, sr=sc, n=n))
-        yield
+            if i == 1:
+                yield
         for it in range(ITERS):
             last = it == ITERS - 1
             rows_here = HD if last else 2 * HD
@@ -372,11 +373,6 @@
     def _():
         pl.semaphore_signal(ready, inc=1, device_id=(s - 16, c), device_id_type=MESH)
 
-    send_tail(0)
-    for g in range(1, PAIRS):
-        gram_stage(g)
-        send_tail(g)
-    VAL.wait()
     def send_early(st):
         @pl.when(c == 0)
         def _():
@@ -387,21 +383,30 @@
         def _():
             send_tail(st)
 
+    send_tail(0)
+    for g in range(1, PAIRS):
+        gram_stage(g)
+        send_early(g)
+        if g > 1:
+            send_late(g - 1)
+    VAL.wait()
     for st in range(PAIRS, STAGES):
         cross_stage(st)
         send_early(st)
+        if st == PAIRS:
+            send_late(PAIRS - 1)
     row_sum(0)
+    row_sum(1)
     send_late(4)
-    row_sum(1)
-    send_late(5)
     QUERY.wait()
     prepare(0)
     row_sum(2)
+    send_late(5)
+    row_sum(3)
     send_late(6)
-    row_sum(3)
+    prepare(1)
     send_late(7)
     send_late(8)
-    prepare(1)
     row_sum(4)
     plane_sum(0)
     plane_sum(1)
@@ -413,15 +418,16 @@
     give_back(1)
     prepare(2)
     row_sum(7)
-    give_back(2)
     row_sum(8)
     plane_sum(4)
+    give_back(2)
     prepare(3)
+    plane_sum(5)
     give_back(3)
-    plane_sum(5)
+    first = solve((0, 1))
+    next(first)
     plane_sum(6)
     give_back(4)
-    first = solve((0, 1))
     next(first)
     next(first)
     give_back(5)
@@ -433,6 +439,7 @@
     for _ in first:
         pass
     second = solve((2, 3))
+    next(second)
     next(second)
     give_back(7)
     give_back(8)

time: 31.5 us -> 31.3 us (level)
  no operation moved by 1% of the time
where the time goes in v7:
time: 31.3 us
  Pallas kernels  30.5 us (97%)
  local copies, waits for them, and re-layouts  0.71 us (2%)
    pallas_call x1, Pallas kernels, on_device(): pl.pallas_call(kernel, out_shape=pltpu.VMEM((TOK, half), BF16), in_specs=...  30.5 us
    unnamed x1, local copies, waits for them, and re-layouts  0.71 us

profile of v7, /device:TPU:225, one launch (start us, length us, event | category | flops | bytes accessed | tf_op | source)
XLA Modules:
  0.0 31.3 jit_solution(3976912311005258554)
XLA Ops:
  0.0 30.5 %mesa.1 = bf16[128,1024]{1,0:T(8,128)(2,1)S(1)} custom-call(bf16[128,1024]{1,0:T(8,128)(2,1)} %q_hbm.1, bf16[128,1024]{1,0:T(8,128)(2,1)} %k_hbm.1, bf16[128,1024]{1,0:T(8,128)(2,1)} %v_hbm.1, s32[1,128]{1,0:T(1,128)} %bitcast.2, f32[1,128]{1,0:T(1,128)} %bitcast.3, bf16[1024,2048]{1,0:T(8,128)(2,1)} %w_hbm.1), custom_call_target="tpu_custom_call" | custom-call | tf_op jit(solution)/shard_map/mesa/pallas_call | solution.py:490
  30.6 0.7 %copy.8 = bf16[128,1024]{1,0:T(8,128)(2,1)} copy(bf16[128,1024]{1,0:T(8,128)(2,1)S(1)} %mesa.1) | data formatting | bytes 524288

commit v8 on v7

--- a/solution.py
+++ b/solution.py
@@ -18,6 +18,7 @@
 CROSS = ((0, 1), (2, 3), (4, 5), (6,), (7,))
 STAGES = PAIRS + len(CROSS)
 LAST = 7
+TURN = 4
 NB = 4
 epsilon = 1e-06
 damping = 1.0
@@ -64,9 +65,17 @@
         pl.semaphore_signal(barrier, inc=1, device_id=(at_x(d), c), device_id_type=MESH)
     pl.semaphore_signal(barrier, inc=1, device_id=(s, 1 - c), device_id_type=MESH)
 
-    @pl.when(z < LAST)
+    @pl.when(z < TURN)
     def _():
-        pl.semaphore_signal(barrier, inc=1, device_id=(s + 16, c), device_id_type=MESH)
+        pl.semaphore_signal(
+            barrier, inc=1, device_id=(lax.rem(s + 16, 128), c), device_id_type=MESH
+        )
+
+    @pl.when(z > TURN)
+    def _():
+        pl.semaphore_signal(
+            barrier, inc=1, device_id=(lax.rem(s + 112, 128), c), device_id_type=MESH
+        )
 
     loads = [
         pltpu.make_async_copy(a, b, lsem.at[i])
@@ -233,10 +242,14 @@
             total = total + wt(WZ + i) * rbuf[st, i, r]
         zs[st, r] = total
 
+        if st == 0:
+
+            @pl.when(z < TURN)
+            def _():
+                pl.semaphore_wait(ready, 1)
+
         @pl.when(z < LAST)
         def _():
-            if st == 0:
-                pl.semaphore_wait(ready, 1)
             zcopy(st).start()
 
     def give_back(st):
@@ -367,11 +380,14 @@
 
     KEY.wait()
     gram_stage(0)
-    pl.semaphore_wait(barrier, 7 + jnp.minimum(z, 1))
-
-    @pl.when(z > 0)
+    greeted = jnp.where((z > 0) & (z <= TURN), 1, 0) + jnp.where((z >= TURN) & (z < LAST), 1, 0)
+    pl.semaphore_wait(barrier, 7 + greeted)
+
+    @pl.when((z > 0) & (z <= TURN))
     def _():
-        pl.semaphore_signal(ready, inc=1, device_id=(s - 16, c), device_id_type=MESH)
+        pl.semaphore_signal(
+            ready, inc=1, device_id=(lax.rem(s + 112, 128), c), device_id_type=MESH
+        )
 
     def send_early(st):
         @pl.when(c == 0)
@@ -386,27 +402,23 @@
     send_tail(0)
     for g in range(1, PAIRS):
         gram_stage(g)
-        send_early(g)
-        if g > 1:
-            send_late(g - 1)
+        send_tail(g)
     VAL.wait()
     for st in range(PAIRS, STAGES):
         cross_stage(st)
         send_early(st)
-        if st == PAIRS:
-            send_late(PAIRS - 1)
     row_sum(0)
+    send_late(4)
     row_sum(1)
-    send_late(4)
+    send_late(5)
     QUERY.wait()
     prepare(0)
     row_sum(2)
-    send_late(5)
+    send_late(6)
     row_sum(3)
-    send_late(6)
-    prepare(1)
     send_late(7)
     send_late(8)
+    prepare(1)
     row_sum(4)
     plane_sum(0)
     plane_sum(1)

time: 31.3 us -> 31.3 us (level)
  no operation moved by 1% of the time
where the time goes in v8:
time: 31.3 us; the launch traced here: 31.2 us
  Pallas kernels  30.5 us (97%)
  local copies, waits for them, and re-layouts  0.71 us (2%)
    pallas_call x1, Pallas kernels, on_device(): pl.pallas_call(kernel, out_shape=pltpu.VMEM((TOK, half), BF16), in_specs=...  30.5 us
    unnamed x1, local copies, waits for them, and re-layouts  0.71 us

profile of v8, /device:TPU:225, one launch (start us, length us, event | category | flops | bytes accessed | tf_op | source)
XLA Modules:
  0.0 31.2 jit_solution(11193895939427777962)
XLA Ops:
  0.0 30.5 %mesa.1 = bf16[128,1024]{1,0:T(8,128)(2,1)S(1)} custom-call(bf16[128,1024]{1,0:T(8,128)(2,1)} %q_hbm.1, bf16[128,1024]{1,0:T(8,128)(2,1)} %k_hbm.1, bf16[128,1024]{1,0:T(8,128)(2,1)} %v_hbm.1, s32[1,128]{1,0:T(1,128)} %bitcast.2, f32[1,128]{1,0:T(1,128)} %bitcast.3, bf16[1024,2048]{1,0:T(8,128)(2,1)} %w_hbm.1), custom_call_target="tpu_custom_call" | custom-call | tf_op jit(solution)/shard_map/mesa/pallas_call | solution.py:502
  30.5 0.7 %copy.8 = bf16[128,1024]{1,0:T(8,128)(2,1)} copy(bf16[128,1024]{1,0:T(8,128)(2,1)S(1)} %mesa.1) | data formatting | bytes 524288

commit v9 on v8

--- a/solution.py
+++ b/solution.py
@@ -402,23 +402,27 @@
     send_tail(0)
     for g in range(1, PAIRS):
         gram_stage(g)
-        send_tail(g)
+        send_early(g)
+        if g > 1:
+            send_late(g - 1)
     VAL.wait()
     for st in range(PAIRS, STAGES):
         cross_stage(st)
         send_early(st)
+        if st == PAIRS:
+            send_late(PAIRS - 1)
     row_sum(0)
+    row_sum(1)
     send_late(4)
-    row_sum(1)
-    send_late(5)
     QUERY.wait()
     prepare(0)
     row_sum(2)
+    send_late(5)
+    row_sum(3)
     send_late(6)
-    row_sum(3)
+    prepare(1)
     send_late(7)
     send_late(8)
-    prepare(1)
     row_sum(4)
     plane_sum(0)
     plane_sum(1)

time: 31.3 us -> 31.3 us (level)
  no operation moved by 1% of the time
where the time goes in v9:
time: 31.3 us
  Pallas kernels  30.5 us (97%)
  local copies, waits for them, and re-layouts  0.71 us (2%)
    pallas_call x1, Pallas kernels, on_device(): pl.pallas_call(kernel, out_shape=pltpu.VMEM((TOK, half), BF16), in_specs=...  30.5 us
    unnamed x1, local copies, waits for them, and re-layouts  0.71 us

profile of v9, /device:TPU:225, one launch (start us, length us, event | category | flops | bytes accessed | tf_op | source)
XLA Modules:
  0.0 31.3 jit_solution(9590564122399970665)
XLA Ops:
  0.0 30.5 %mesa.1 = bf16[128,1024]{1,0:T(8,128)(2,1)S(1)} custom-call(bf16[128,1024]{1,0:T(8,128)(2,1)} %q_hbm.1, bf16[128,1024]{1,0:T(8,128)(2,1)} %k_hbm.1, bf16[128,1024]{1,0:T(8,128)(2,1)} %v_hbm.1, s32[1,128]{1,0:T(1,128)} %bitcast.2, f32[1,128]{1,0:T(1,128)} %bitcast.3, bf16[1024,2048]{1,0:T(8,128)(2,1)} %w_hbm.1), custom_call_target="tpu_custom_call" | custom-call | tf_op jit(solution)/shard_map/mesa/pallas_call | solution.py:506
  30.5 0.7 %copy.8 = bf16[128,1024]{1,0:T(8,128)(2,1)} copy(bf16[128,1024]{1,0:T(8,128)(2,1)S(1)} %mesa.1) | data formatting | bytes 524288
